TPU v7x, 128 devices: a whole 4x4x4 slice. The times are simulated.
128 devices in a mesh: leaf: 32 (over y, x, core), probe: 4 (over z).
Axes of the slice: x: 4, y: 4, z: 4, core: 2. Of those that a mesh axis runs over, the one named last changes fastest.
Arguments:
- points: bfloat16 [131072, 2048], P('leaf', 'probe'), parts along dimension 1, may hold values from -6 to 6
- leaf_basis: bfloat16 [512, 64, 256], P('leaf'), may hold values from -0.375 to 0.375
- local_transfer: bfloat16 [960, 4096], P('leaf'), may hold values from -0.5 to 0.5
- top_transfer: bfloat16 [62, 4096], replicated, may hold values from -0.5 to 0.5
- sources: int32 [32736], P('leaf'), may hold values from 0 to 511, as said below
- couplings: bfloat16 [32736, 4096], P('leaf'), as said below
Outputs:
- coupled: bfloat16 [992, 64, 2048], P('leaf', None, 'probe'), parts along dimension 2
- ancestors: bfloat16 [32, 5, 64, 2048], P('leaf', None, None, 'probe'), parts along dimension 3
There are 4 independent parts, one for each index of `probe`. A program takes and returns all parts, laid end to end along the dimension named above; an argument that names none is the same for every part. Nothing has to cross between parts.
Inputs may be any that keep to these rules, and one draw needn't show every extreme that they name: `sources`: each entry names a cluster of its target's level lying in the target's subtree or in one of the two subtrees on either side; the entries of one target are distinct. `couplings`: tiles of level h have entries of deviation (3 * 64 * 16 / 2^h)^(-1/2).
All inputs are finite; a program needn't handle non-finite values.
Results may differ from a plain program's by a relative error of at most 0.0095.
Values may be sent and summed in bfloat16 or wider, within the bound.
No kernel may reach another device: no remote copies, remote signals or barrier semaphores. Data moves between devices by JAX's collectives and lax.ppermute only.
A program may use at most 128 MiB of HBM per device.

v0:
```python
import jax
import jax.numpy as jnp
from jax import lax
from jax.sharding import PartitionSpec as P

LEAF = 256
RANK = 64
PROBES = 512
LOCAL = 5
LEAF_DEV = 16


def from_behind(block, axis, distance):
    devices = range(lax.axis_size(axis))
    route = [(i - distance, i) for i in devices if i - distance in devices]
    return lax.ppermute(block, axis, route)


def joined_along(tiles, dim):
    tiles = jnp.moveaxis(tiles, 0, dim)
    lengths = tiles.shape
    return tiles.reshape(*lengths[:dim], lengths[dim] * lengths[dim + 1], *lengths[dim + 2 :])


def copy_for_each(value, axis):
    copies = jnp.broadcast_to(value, (lax.axis_size(axis), *value.shape))
    return lax.all_to_all(copies, axis, split_axis=0, concat_axis=0, tiled=True)


def gathered_copies(value, axis, dim):
    return joined_along(copy_for_each(value, axis), dim)


def lift_level(children, matrices):
    shaped = matrices.reshape(-1, RANK, RANK)
    products = jnp.einsum("cab,cap->cbp", shaped, children, preferred_element_type=jnp.float32)
    return products.reshape(-1, 2, RANK, PROBES).sum(axis=1)


def couple_level(window, level_sources, level_tiles, anchor, number):
    local_index = (level_sources - anchor).reshape(number, 3 * number)
    slots = jnp.arange(5 * number, dtype=jnp.int32)
    selector = (local_index[:, :, None] == slots[None, None, :]).astype(jnp.bfloat16)
    tiles = level_tiles.reshape(number, 3 * number, RANK * RANK)
    placed = jnp.einsum("tks,tkm->tsm", selector, tiles, preferred_element_type=jnp.float32)
    dense = placed.astype(jnp.bfloat16).reshape(number, 5 * number, RANK, RANK)
    summed = jnp.einsum("tsab,sap->tbp", dense, window, preferred_element_type=jnp.float32)
    return summed.astype(jnp.bfloat16)


def joint_window(joined):
    pieces = []
    for distance in (2, 1, 0, -1, -2):
        if distance == 0:
            pieces.append(joined)
        else:
            pieces.append(from_behind(joined, "leaf", distance))
    return pieces


def shards(points, leaf_basis, local_transfer, top_transfer, sources, couplings):
    device = lax.axis_index("leaf")
    subtrees = lax.axis_size("leaf")
    levels_up = subtrees.bit_length() - 1
    blocks = points.reshape(LEAF_DEV, LEAF, PROBES)
    first = jnp.einsum("jrl,jlp->jrp", leaf_basis, blocks, preferred_element_type=jnp.float32)
    moments = [first.astype(jnp.bfloat16)]
    cursor = 0
    for height in range(1, LOCAL):
        number = LEAF_DEV >> height - 1
        lifted = lift_level(moments[-1], local_transfer[cursor : cursor + number])
        moments.append(lifted.astype(jnp.bfloat16))
        cursor += number
    windows = []
    received = joint_window(jnp.concatenate(moments, axis=0))
    cursor = 0
    for height in range(LOCAL):
        number = LEAF_DEV >> height
        windows.append(
            jnp.concatenate([piece[cursor : cursor + number] for piece in received], axis=0)
        )
        cursor += number
    outputs = []
    cursor = 0
    for height in range(LOCAL):
        number = LEAF_DEV >> height
        entries = 3 * number * number
        anchor = (device - 2) * number
        outputs.append(
            couple_level(
                windows[height],
                sources[cursor : cursor + entries],
                couplings[cursor : cursor + entries],
                anchor,
                number,
            )
        )
        cursor += entries
    coupled = jnp.concatenate(outputs, axis=0)
    device_root = moments[LOCAL - 1]
    ladder = []
    current = gathered_copies(device_root, "leaf", 0)
    cursor = 0
    for height in range(levels_up):
        clusters = current.shape[0]
        current = lift_level(current, top_transfer[cursor : cursor + clusters]).astype(jnp.bfloat16)
        cursor += clusters
        ladder.append(lax.dynamic_index_in_dim(current, device >> height + 1, 0, keepdims=False))
    ancestors = jnp.stack(ladder, axis=0)[None]
    return (coupled, ancestors)


def solution(mesh):
    placed = (
        P("leaf", "probe"),
        P("leaf", None, None),
        P("leaf", None),
        P(),
        P("leaf"),
        P("leaf", None),
    )
    return jax.shard_map(
        shards,
        mesh=mesh,
        in_specs=placed,
        out_specs=(P("leaf", None, "probe"), P("leaf", None, None, "probe")),
        check_vma=False,
    )
```

profile of v0, /device:TPU:103, one launch (start us, length us, event | category | flops | bytes accessed | tf_op | source)
XLA Modules:
  0.0 156.7 jit_solution(4520521494450720305)
XLA Ops:
  3.8 4.0 %constant_dynamic-update-slice_fusion.4 = (bf16[31,64,512]{2,1,0:T(8,128)(2,1)}, bf16[16,64,512]{2,1,0:T(8,128)(2,1)S(1)}) fusion(bf16[16,64,256]{2,1,0:T(8,128)(2,1)S(1)} %copy-done, bf16[16,256,512]{2,1,0:T(8,128)(2,1)} %bitcast.169), kind=kOutput, calls=%fused_computation.66 | convolution fusion | flops 268959744 | bytes 6815744 | tf_op jit(solution)/shard_map/jrl,jlp->jrp/dot_general | solution.py:66
  13.2 3.1 %collective-permute-start = (bf16[31,64,512]{2,1,0:T(8,128)(2,1)}, bf16[31,64,512]{2,1,0:T(8,128)(2,1)}, u32[]{:S(2)}, u32[]{:S(2)}) collective-permute-start(bf16[31,64,512]{2,1,0:T(8,128)(2,1)} %get-tuple-element.4), channel_id=1, source_target_pairs={{0,8},{4,12},{8,16},{12,20},{16,24},{20,28},{24,32},{28,36},{32,40... | collective-permute-start | bytes 6094856 | tf_op jit(solution)/shard_map/ppermute | solution.py:16
  16.4 4.0 %collective-permute-start.1 = (bf16[31,64,512]{2,1,0:T(8,128)(2,1)}, bf16[31,64,512]{2,1,0:T(8,128)(2,1)}, u32[]{:S(2)}, u32[]{:S(2)}) collective-permute-start(bf16[31,64,512]{2,1,0:T(8,128)(2,1)} %get-tuple-element.4), channel_id=1, source_target_pairs={{0,4},{4,8},{8,12},{12,16},{16,20},{20,24},{24,28},{28,32},{32,36}... | collective-permute-start | bytes 6094856 | tf_op jit(solution)/shard_map/ppermute | solution.py:16
  20.3 1.9 %collective-permute-start.2 = (bf16[31,64,512]{2,1,0:T(8,128)(2,1)}, bf16[31,64,512]{2,1,0:T(8,128)(2,1)}, u32[]{:S(2)}, u32[]{:S(2)}) collective-permute-start(bf16[31,64,512]{2,1,0:T(8,128)(2,1)} %get-tuple-element.4), channel_id=1, source_target_pairs={{4,0},{8,4},{12,8},{16,12},{20,16},{24,20},{28,24},{32,28},{36,32}... | collective-permute-start | bytes 6094856 | tf_op jit(solution)/shard_map/ppermute | solution.py:16
  22.3 2.2 %collective-permute-start.3 = (bf16[31,64,512]{2,1,0:T(8,128)(2,1)}, bf16[31,64,512]{2,1,0:T(8,128)(2,1)}, u32[]{:S(2)}, u32[]{:S(2)}) collective-permute-start(bf16[31,64,512]{2,1,0:T(8,128)(2,1)} %get-tuple-element.4), channel_id=1, source_target_pairs={{8,0},{12,4},{16,8},{20,12},{24,16},{28,20},{32,24},{36,28},{40,32... | collective-permute-start | bytes 6094856 | tf_op jit(solution)/shard_map/ppermute | solution.py:16
  24.4 1.5 broadcast_in_dim.4
  26.0 9.0 %all-to-all-start = ((bf16[32,1,64,512]{3,2,1,0:T(8,128)(2,1)}), bf16[32,1,64,512]{3,2,1,0:T(8,128)(2,1)}, u32[]{:S(2)}, u32[]{:S(2)}) async-start(bf16[32,1,64,512]{3,2,1,0:T(8,128)(2,1)} %broadcast_in_dim.4), calls=%async_computation | async-start | bytes 4194304 | tf_op jit(solution)/shard_map/all_to_all | solution.py:27
  35.0 6.2 %slice.118 = bf16[768,4096]{1,0:T(8,128)(2,1)} slice(bf16[1023,4096]{1,0:T(8,128)(2,1)} %param.11), slice={[0:768], [0:4096]} | slice | bytes 12582912 | tf_op jit(solution)/shard_map/slice | solution.py:93
  41.3 9.7 %convolution_convert_fusion = bf16[16,80,4096]{2,1,0:T(8,128)(2,1)} fusion(bf16[16,48,4096]{2,1,0:T(8,128)(2,1)} %bitcast.165, s32[16,48]{1,0:T(8,128)S(1)} %sub.68), kind=kOutput, calls=%fused_computation | convolution fusion | flops 508620800 | bytes 16780288 | tf_op jit(solution)/shard_map/tks,tkm->tsm/dot_general | solution.py:45
  51.1 2.7 %slice.128 = bf16[192,4096]{1,0:T(8,128)(2,1)} slice(bf16[1023,4096]{1,0:T(8,128)(2,1)} %param.11), slice={[768:960], [0:4096]} | slice | bytes 3145728 | tf_op jit(solution)/shard_map/slice | solution.py:93
  53.8 29.3 %reshape.167 = bf16[16,80,64,64]{3,2,1,0:T(8,128)(2,1)} reshape(bf16[16,80,4096]{2,1,0:T(8,128)(2,1)} %convolution_convert_fusion) | data formatting | bytes 20971520 | tf_op jit(solution)/shard_map/reshape | solution.py:46
  83.2 2.4 %convolution_convert_fusion.1 = bf16[8,40,4096]{2,1,0:T(8,128)(2,1)S(1)} fusion(bf16[8,24,4096]{2,1,0:T(8,128)(2,1)} %bitcast.166, s32[8,24]{1,0:T(8,128)S(1)} %sub.71), kind=kOutput, calls=%fused_computation.1 | convolution fusion | flops 64232960 | bytes 4195072 | tf_op jit(solution)/shard_map/tks,tkm->tsm/dot_general | solution.py:45
  85.6 6.7 %reshape.177 = bf16[8,40,64,64]{3,2,1,0:T(8,128)(2,1)} reshape(bf16[8,40,4096]{2,1,0:T(8,128)(2,1)S(1)} %convolution_convert_fusion.1) | data formatting | bytes 5242880 | tf_op jit(solution)/shard_map/reshape | solution.py:46
  104.2 1.7 %slice_dynamic-update-slice_fusion.11 = bf16[20,64,512]{2,1,0:T(8,128)(2,1)} fusion(bf16[31,64,512]{2,1,0:T(8,128)(2,1)} %collective-permute-done), kind=kLoop, calls=%fused_computation.55 | loop fusion | bytes 524288
  105.9 1.7 %slice_dynamic-update-slice_fusion.10 = bf16[20,64,512]{2,1,0:T(8,128)(2,1)} fusion(bf16[20,64,512]{2,1,0:T(8,128)(2,1)} %slice_dynamic-update-slice_fusion.11, bf16[31,64,512]{2,1,0:T(8,128)(2,1)} %collective-permute-done.1), kind=kLoop, calls=%fused_computation.54 | loop fusion | bytes 524288
  108.3 1.9 %slice_dynamic-update-slice_fusion.7 = bf16[40,64,512]{2,1,0:T(8,128)(2,1)} fusion(bf16[31,64,512]{2,1,0:T(8,128)(2,1)} %collective-permute-done), kind=kLoop, calls=%fused_computation.48 | loop fusion | bytes 1048576
  110.2 9.0 %all-to-all-done = bf16[32,1,64,512]{3,2,1,0:T(8,128)(2,1)} async-done(((bf16[32,1,64,512]{3,2,1,0:T(8,128)(2,1)}), bf16[32,1,64,512]{3,2,1,0:T(8,128)(2,1)}, u32[]{:S(2)}, u32[]{:S(2)}) %all-to-all-start) | async-done | bytes 2097184 | tf_op jit(solution)/shard_map/all_to_all | solution.py:27
  119.2 2.6 %bitcast_reduce_fusion = bf16[16,64,512]{2,1,0:T(8,128)(2,1)S(1)} fusion(bf16[32,64,64]{2,1,0:T(8,128)(2,1)S(1)} %reshape.184, bf16[32,1,64,512]{3,2,1,0:T(8,128)(2,1)} %all-to-all-done), kind=kOutput, calls=%fused_computation.7 | convolution fusion | flops 134742016 | bytes 3407872 | tf_op jit(solution)/shard_map/cab,cap->cbp/dot_general | solution.py:36
  129.3 1.4 slice_dynamic-update-slice_fusion
  130.7 10.4 %fusion.8 = bf16[31,64,512]{2,1,0:T(8,128)(2,1)S(1)} fusion(bf16[16,80,64,64]{3,2,1,0:T(8,128)(2,1)} %reshape.167, bf16[80,64,512]{2,1,0:T(8,128)(2,1)S(1)} %slice_dynamic-update-slice_fusion), kind=kOutput, calls=%fused_computation.16 | convolution fusion | flops 5369233408 | bytes 16777216 | tf_op jit(solution)/shard_map/tsab,sap->tbp/dot_general | solution.py:47
  144.4 1.5 fusion.21
  146.0 1.8 %slice_dynamic-update-slice_fusion.9 = bf16[20,64,512]{2,1,0:T(8,128)(2,1)} fusion(bf16[20,64,512]{2,1,0:T(8,128)(2,1)} %constant_dynamic-update-slice_fusion.7, bf16[31,64,512]{2,1,0:T(8,128)(2,1)} %collective-permute-done.2), kind=kLoop, calls=%fused_computation.53 | loop fusion | bytes 524288
  147.7 1.7 %slice_dynamic-update-slice_fusion.8 = bf16[20,64,512]{2,1,0:T(8,128)(2,1)} fusion(bf16[20,64,512]{2,1,0:T(8,128)(2,1)} %slice_dynamic-update-slice_fusion.9, bf16[31,64,512]{2,1,0:T(8,128)(2,1)} %collective-permute-done.3), kind=kLoop, calls=%fused_computation.52 | loop fusion | bytes 524288 | tf_op jit(solution)/shard_map/concatenate | solution.py:80
  149.5 1.8 %fusion.30 = bf16[31,64,512]{2,1,0:T(8,128)(2,1)S(1)} fusion(bf16[31,64,512]{2,1,0:T(8,128)(2,1)S(1)} %fusion.21, bf16[4,20,64,64]{3,2,1,0:T(8,128)(2,1)S(1)} %reshape.204, bf16[20,64,512]{2,1,0:T(8,128)(2,1)} %slice_dynamic-update-slice_fusion.8), kind=kOutput, calls=%fused_computation.24 | convolution fusion | flops 335675392 | bytes 2883584 | tf_op jit(solution)/shard_map/tsab,sap->tbp/dot_general | solution.py:47
  (123 shorter events, 37.1 us)
Async XLA Ops:
  0.6 3.1 %copy-start = (bf16[16,64,256]{2,1,0:T(8,128)(2,1)S(1)}, bf16[16,64,256]{2,1,0:T(8,128)(2,1)}, u32[]{:S(2)}) copy-start(bf16[16,64,256]{2,1,0:T(8,128)(2,1)} %param.7) | copy-start | bytes 1572868
  9.3 16.7 %copy-start.4 = (bf16[8,64,512]{2,1,0:T(8,128)(2,1)}, bf16[8,64,512]{2,1,0:T(8,128)(2,1)S(1)}, u32[]{:S(2)}) copy-start(bf16[8,64,512]{2,1,0:T(8,128)(2,1)S(1)} %bitcast_reduce_fusion.2) | copy-start | bytes 1572868
  13.2 11.2 %copy-start.9 = (bf16[512,64]{0,1:T(8,128)(2,1)}, bf16[512,64]{0,1:T(8,128)(2,1)S(1)}, u32[]{:S(2)}) copy-start(bf16[512,64]{0,1:T(8,128)(2,1)S(1)} %get-tuple-element.5) | copy-start | bytes 196612
  13.2 88.3 %collective-permute-start = (bf16[31,64,512]{2,1,0:T(8,128)(2,1)}, bf16[31,64,512]{2,1,0:T(8,128)(2,1)}, u32[]{:S(2)}, u32[]{:S(2)}) collective-permute-start(bf16[31,64,512]{2,1,0:T(8,128)(2,1)} %get-tuple-element.4), channel_id=1, source_target_pairs={{0,8},{4,12},{8,16},{12,20},{16,24},{20,28},{24,32},{28,36},{32,40... | collective-permute-start | bytes 6094856 | tf_op jit(solution)/shard_map/ppermute | solution.py:16
  16.4 86.1 %collective-permute-start.1 = (bf16[31,64,512]{2,1,0:T(8,128)(2,1)}, bf16[31,64,512]{2,1,0:T(8,128)(2,1)}, u32[]{:S(2)}, u32[]{:S(2)}) collective-permute-start(bf16[31,64,512]{2,1,0:T(8,128)(2,1)} %get-tuple-element.4), channel_id=1, source_target_pairs={{0,4},{4,8},{8,12},{12,16},{16,20},{20,24},{24,28},{28,32},{32,36}... | collective-permute-start | bytes 6094856 | tf_op jit(solution)/shard_map/ppermute | solution.py:16
  20.3 107.6 %collective-permute-start.2 = (bf16[31,64,512]{2,1,0:T(8,128)(2,1)}, bf16[31,64,512]{2,1,0:T(8,128)(2,1)}, u32[]{:S(2)}, u32[]{:S(2)}) collective-permute-start(bf16[31,64,512]{2,1,0:T(8,128)(2,1)} %get-tuple-element.4), channel_id=1, source_target_pairs={{4,0},{8,4},{12,8},{16,12},{20,16},{24,20},{28,24},{32,28},{36,32}... | collective-permute-start | bytes 6094856 | tf_op jit(solution)/shard_map/ppermute | solution.py:16
  22.3 107.0 %collective-permute-start.3 = (bf16[31,64,512]{2,1,0:T(8,128)(2,1)}, bf16[31,64,512]{2,1,0:T(8,128)(2,1)}, u32[]{:S(2)}, u32[]{:S(2)}) collective-permute-start(bf16[31,64,512]{2,1,0:T(8,128)(2,1)} %get-tuple-element.4), channel_id=1, source_target_pairs={{8,0},{12,4},{16,8},{20,12},{24,16},{28,20},{32,24},{36,28},{40,32... | collective-permute-start | bytes 6094856 | tf_op jit(solution)/shard_map/ppermute | solution.py:16
  26.0 93.2 %all-to-all-start = ((bf16[32,1,64,512]{3,2,1,0:T(8,128)(2,1)}), bf16[32,1,64,512]{3,2,1,0:T(8,128)(2,1)}, u32[]{:S(2)}, u32[]{:S(2)}) async-start(bf16[32,1,64,512]{3,2,1,0:T(8,128)(2,1)} %broadcast_in_dim.4), calls=%async_computation | async-start | bytes 4194304 | tf_op jit(solution)/shard_map/all_to_all | solution.py:27
  35.0 6.3 %copy-start.15 = (s32[1023]{0:T(1024)S(1)}, s32[1023]{0:T(1024)}, u32[]{:S(2)}) copy-start(s32[1023]{0:T(1024)} %param.10) | copy-start | bytes 12280
  51.0 2.7 %copy-start.6 = (bf16[62,4096]{1,0:T(8,128)(2,1)S(1)}, bf16[62,4096]{1,0:T(8,128)(2,1)}, u32[]{:S(2)}) copy-start(bf16[62,4096]{1,0:T(8,128)(2,1)} %param.9) | copy-start | bytes 1523716
  85.5 6.8 %slice-start = ((bf16[1023,4096]{1,0:T(8,128)(2,1)}), bf16[48,4096]{1,0:T(8,128)(2,1)S(1)}, s32[]{:S(2)}) async-start(bf16[1023,4096]{1,0:T(8,128)(2,1)} %param.11), calls=%async_computation.1 | async-start | bytes 786432 | tf_op jit(solution)/shard_map/slice | solution.py:93
  92.3 3.1 %slice-start.1 = ((bf16[1023,4096]{1,0:T(8,128)(2,1)}), bf16[12,4096]{1,0:T(8,128)(2,1)S(1)}, s32[]{:S(2)}) async-start(bf16[1023,4096]{1,0:T(8,128)(2,1)} %param.11), calls=%async_computation.2 | async-start | bytes 262144 | tf_op jit(solution)/shard_map/slice | solution.py:93
  93.9 5.1 %slice-start.4 = ((bf16[62,4096]{1,0:T(8,128)(2,1)}), bf16[32,4096]{1,0:T(8,128)(2,1)S(1)}, s32[]{:S(2)}) async-start(bf16[62,4096]{1,0:T(8,128)(2,1)} %param.9), calls=%async_computation.5 | async-start | bytes 524288 | tf_op jit(solution)/shard_map/slice | solution.py:106
  93.9 5.6 %slice-start.5 = ((bf16[62,4096]{1,0:T(8,128)(2,1)}), bf16[16,4096]{1,0:T(8,128)(2,1)S(1)}, s32[]{:S(2)}) async-start(bf16[62,4096]{1,0:T(8,128)(2,1)} %param.9), calls=%async_computation.6 | async-start | bytes 262144 | tf_op jit(solution)/shard_map/slice | solution.py:106
  93.9 5.9 %slice-start.6 = ((bf16[62,4096]{1,0:T(8,128)(2,1)}), bf16[8,4096]{1,0:T(8,128)(2,1)S(1)}, s32[]{:S(2)}) async-start(bf16[62,4096]{1,0:T(8,128)(2,1)} %param.9), calls=%async_computation.7 | async-start | bytes 131072 | tf_op jit(solution)/shard_map/slice | solution.py:106
  93.9 6.7 %slice-start.7 = ((bf16[62,4096]{1,0:T(8,128)(2,1)}), bf16[4,4096]{1,0:T(4,128)(2,1)S(1)}, s32[]{:S(2)}) async-start(bf16[62,4096]{1,0:T(8,128)(2,1)} %param.9), calls=%async_computation.8 | async-start | bytes 65536 | tf_op jit(solution)/shard_map/slice | solution.py:106
  110.2 12.7 %copy-start.5 = (bf16[8,64,512]{2,1,0:T(8,128)(2,1)S(1)}, bf16[8,64,512]{2,1,0:T(8,128)(2,1)}, u32[]{:S(2)}) copy-start(bf16[8,64,512]{2,1,0:T(8,128)(2,1)} %copy-done.4) | copy-start | bytes 1572868
  129.2 15.1 %slice-start.2 = ((s8[5242880]{0:T(1024)(128)(4,1)}), s8[4194304]{0:T(1024)(128)(4,1)S(1)}, s32[]{:S(2)}) async-start(s8[5242880]{0:T(1024)(128)(4,1)} %bitcast.167), calls=%async_computation.3 | async-start | bytes 8388608
  130.7 10.5 %copy-start.11 = (bf16[8,64,64]{2,1,0:T(8,128)(2,1)S(1)}, bf16[8,64,64]{2,1,0:T(8,128)(2,1)}, u32[]{:S(2)}) copy-start(bf16[8,64,64]{2,1,0:T(8,128)(2,1)} %reshape.188) | copy-start | bytes 196612
  130.7 10.8 %copy-start.12 = (bf16[4,64,64]{2,1,0:T(8,128)(2,1)S(1)}, bf16[4,64,64]{2,1,0:T(8,128)(2,1)}, u32[]{:S(2)}) copy-start(bf16[4,64,64]{2,1,0:T(8,128)(2,1)} %reshape.190) | copy-start | bytes 98308
  130.7 13.7 %slice-start.3 = ((s8[5242880]{0:T(1024)(128)(4,1)}), s8[1048576]{0:T(1024)(128)(4,1)S(1)}, s32[]{:S(2)}) async-start(s8[5242880]{0:T(1024)(128)(4,1)} %bitcast.167), calls=%async_computation.4 | async-start | bytes 2097152
  142.1 3.9 %copy-start.14 = (bf16[5,64,512]{2,1,0:T(8,128)(2,1)}, bf16[5,64,512]{2,1,0:T(8,128)(2,1)S(1)}, u32[]{:S(2)}) copy-start(bf16[5,64,512]{2,1,0:T(8,128)(2,1)S(1)} %fusion.39) | copy-start | bytes 983044
  146.0 5.4 %copy-start.8 = (bf16[10,64,512]{2,1,0:T(8,128)(2,1)S(1)}, bf16[10,64,512]{2,1,0:T(8,128)(2,1)}, u32[]{:S(2)}) copy-start(bf16[10,64,512]{2,1,0:T(8,128)(2,1)} %copy-done.7) | copy-start | bytes 1966084
  147.7 8.9 %copy-start.1 = (bf16[16,64,256]{2,1,0:T(8,128)(2,1)S(1)}, bf16[16,64,256]{2,1,0:T(8,128)(2,1)}, u32[]{:S(2)}) copy-start(bf16[16,64,256]{2,1,0:T(8,128)(2,1)} %param.7) | copy-start | bytes 1572868
  (7 other events, 13.4 us)
where the time goes:
time: 159 us; the launch traced here: 157 us
  local copies, waits for them, and re-layouts  85.6 us (54%)
  matrix products  38.3 us (24%)
  starting transfers between devices  20.1 us (13%)
  waiting for transfers between devices  8.98 us (6%)
  other arithmetic  2.3 us (1%)
    reshape x4, local copies, waits for them, and re-layouts, couple_level(): dense = placed.astype(jnp.bfloat16).reshape(number, 5 * number, RANK, RANK)  37.8 us
    unnamed x65, local copies, waits for them, and re-layouts  24.9 us
    dot_general x5, matrix products, couple_level(): jnp.einsum('tsab,sap->tbp', dense, window, preferred_element_type=jnp.flo...  14.3 us
    dot_general x5, matrix products, couple_level(): jnp.einsum('tks,tkm->tsm', selector, tiles, preferred_element_type=jnp.fl...  14.2 us
    ppermute x4, starting transfers between devices, from_behind(): return lax.ppermute(block, axis, route)  11.2 us
    all_to_all x1, starting transfers between devices, copy_for_each(): return lax.all_to_all(copies, axis, split_axis=0, concat_axis=0, tiled=True)  8.99 us
    slice x6, local copies, waits for them, and re-layouts, shards(): couplings[cursor:cursor + entries]  8.99 us
    all_to_all x1, waiting for transfers between devices, copy_for_each(): return lax.all_to_all(copies, axis, split_axis=0, concat_axis=0, tiled=True)  8.97 us
  transfers between devices with their start and end apart: 5, of which 1 were waited for; matrix products, arithmetic and copies ran while one was open for 55% of the time, Pallas kernels for 0%

commit v1 on v0

v1 whole, which is shorter than its diff:
```python
import jax
import jax.numpy as jnp
from jax import lax
from jax.experimental import pallas as pl
from jax.experimental.pallas import tpu as pltpu
from jax.sharding import PartitionSpec as P

LEAF = 256
RANK = 64
PROBES = 512
LOCAL = 5
LEAF_DEV = 16
GROUPS = 32
HALF = 32
BF = jnp.bfloat16
F32 = jnp.float32
COUNTS = (16, 8, 4, 2, 1)
LIFT_ROWS = (0, 512, 768, 896)


def iotas(rows, columns):
    shape = (rows, columns)
    return (
        lax.broadcasted_iota(jnp.int32, shape, 0),
        lax.broadcasted_iota(jnp.int32, shape, 1),
    )


def natural(rank):
    return (rank & 31) * 2 + (rank >> 5)


def ones_where(mask):
    return jnp.where(mask, 1.0, 0.0).astype(BF)


def rank_order():
    row, column = iotas(RANK, RANK)
    return ones_where(column == natural(row))


def rank_order_pair():
    row, column = iotas(2 * RANK, 2 * RANK)
    return ones_where(column == (row & 64) + natural(row & 63))


def identity(size):
    row, column = iotas(size, size)
    return ones_where(row == column)


def group_order():
    row, column = iotas(256, 256)
    return ones_where(column == (row & 15) * 16 + (row >> 4))


def dot(left, right):
    return jnp.dot(left, right, preferred_element_type=F32)


def dot_nt(left, right):
    return lax.dot_general(left, right, (((1,), (1,)), ((), ())), preferred_element_type=F32)


def regrouped(block, order):
    halves = [
        jnp.concatenate(
            [block[:, (16 * half + g) * 128 : (16 * half + g + 1) * 128] for g in range(16)], axis=0
        )
        for half in range(2)
    ]
    return dot(order, jnp.concatenate(halves, axis=1)).astype(BF)


def tile_rows(regroup):
    pieces = []
    for entry in range(16):
        rows = slice(16 * entry, 16 * entry + 16)
        pieces.append(regroup[rows, :128])
        pieces.append(regroup[rows, 128:])
    return jnp.concatenate(pieces, axis=0)


def first_kernel(points_hbm, basis_hbm, links_hbm, out_ref, points_ref, basis_ref, links_ref, sems):
    links_copy = pltpu.make_async_copy(links_hbm, links_ref, sems.at[9])
    links_copy.start()
    basis_copy = pltpu.make_async_copy(basis_hbm, basis_ref, sems.at[8])
    basis_copy.start()
    copies = []
    for k in range(8):
        rows = pl.ds(512 * k, 512)
        copies.append(pltpu.make_async_copy(points_hbm.at[rows], points_ref.at[rows], sems.at[k]))
        copies[-1].start()
    order = group_order()
    flip = rank_order_pair()
    ranks = rank_order()
    links_copy.wait()
    high = jnp.concatenate([links_ref[16:30, :], jnp.zeros((2, 4096), BF)], axis=0)
    for number, block in enumerate((links_ref[0:16, :], high)):
        tiles = tile_rows(regrouped(block, order))
        out_ref[1024 + 128 * number : 1152 + 128 * number, :] = dot_nt(flip, tiles).astype(BF)
    basis_copy.wait()
    for k in range(8):
        basis = jnp.concatenate([basis_ref[2 * k], basis_ref[2 * k + 1]], axis=1)
        basis = dot(ranks, basis).astype(BF)
        copies[k].wait()
        for j in range(2):
            at = 512 * k + LEAF * j
            moment = dot(basis[:, LEAF * j : LEAF * (j + 1)], points_ref[at : at + LEAF, :]).astype(BF)
            to = (2 * k + j) * HALF
            out_ref[to : to + HALF, :] = moment[:HALF]
            out_ref[512 + to : 512 + to + HALF, :] = moment[HALF:]


VMEM_SPEC = pl.BlockSpec(memory_space=pltpu.VMEM)
HBM_SPEC = pl.BlockSpec(memory_space=pl.ANY)


def on_chip(value):
    return pltpu.with_memory_space_constraint(value, pltpu.VMEM)


def off_chip(value):
    return pltpu.with_memory_space_constraint(value, pltpu.HBM)


def limit(mebibytes):
    return pltpu.CompilerParams(vmem_limit_bytes=mebibytes << 20)


def first_moments(points, leaf_basis, local_transfer):
    return pl.pallas_call(
        first_kernel,
        in_specs=[HBM_SPEC] * 3,
        out_specs=VMEM_SPEC,
        out_shape=pltpu.VMEM((1280, PROBES), BF),
        scratch_shapes=[
            pltpu.VMEM((4096, PROBES), BF),
            pltpu.VMEM((LEAF_DEV, RANK, LEAF), BF),
            pltpu.VMEM((30, 4096), BF),
            pltpu.SemaphoreType.DMA((10,)),
        ],
        compiler_params=limit(10),
        name="first_moments",
    )(off_chip(points), off_chip(leaf_basis), off_chip(local_transfer))


def lift_into(packet, upper):
    low_side = lax.broadcasted_iota(jnp.int32, (RANK, 128), 1) < 64
    zero = jnp.zeros((RANK, 128), BF)

    def pair_of_targets(links, lanes, source, start, stride):
        total = None
        for side in range(2):
            left = packet[links + RANK * side : links + RANK * (side + 1), lanes : lanes + 128]
            left = jnp.concatenate(
                [jnp.where(low_side, left, zero), jnp.where(low_side, zero, left)], axis=0
            )
            begin = start + stride * side
            product = dot(left, source[begin : begin + 128, :])
            total = product if total is None else total + product
        return total.astype(BF)

    def keep(moment, base, count, first):
        for j in range(2):
            for side in range(2):
                at = base + side * count * HALF + (first + j) * HALF
                upper[at : at + HALF, :] = moment[j * RANK + side * HALF : j * RANK + (side + 1) * HALF]

    for u in range(4):
        keep(pair_of_targets(1024, 128 * u, packet, 128 * u, 512), 0, 8, 2 * u)
    for u in range(2):
        keep(pair_of_targets(1152, 128 * u, upper, 128 * u, 256), 512, 4, 2 * u)
    keep(pair_of_targets(1152, 256, upper, 512, 128), 768, 2, 0)
    total = None
    for side in range(2):
        left = packet[1152 + RANK * side : 1152 + RANK * (side + 1), 384:448]
        product = dot(left, upper[768 + 64 * side : 768 + 64 * side + 64, :])
        total = product if total is None else total + product
    upper[896:960, :] = total.astype(BF)


def ascend(tops, number, mine, other):
    total = None
    for side in range(2):
        left = tops[RANK * side : RANK * (side + 1), 64 * number : 64 * number + 64]
        rows = slice(HALF * side, HALF * (side + 1))
        product = dot(left, jnp.concatenate([mine[rows], other[rows]], axis=0))
        total = product if total is None else total + product
    return total.astype(BF)


PICKS = (
    (0, 0, 0), (0, 0, 1),
    (32, 1, 0), (32, 1, 1), (32, 1, 2), (32, 1, 3),
    (48, 2, 0), (48, 2, 1),
    (56, 3, 0), (56, 3, 1), (56, 3, 2), (56, 3, 3),
    (60, 4, 0), (60, 4, 1),
)


def lift_kernel(own, near, top_hbm, own_up, near_up, tops, first_top, top_ref, sem):
    copy = pltpu.make_async_copy(top_hbm, top_ref, sem)
    copy.start()
    lift_into(own, own_up)
    lift_into(near, near_up)
    device = lax.axis_index("leaf")
    row, column = iotas(16, 62)
    chosen = jnp.full((16, 62), -1, jnp.int32)
    for number, (begin, shift, flip) in enumerate(PICKS):
        chosen = jnp.where(row == number, begin + ((device >> shift) ^ flip), chosen)
    pick = ones_where(column == chosen)
    copy.wait()
    rows = dot(pick, top_ref[...]).astype(BF)
    tops[...] = dot_nt(rank_order_pair(), tile_rows(regrouped(rows, group_order()))).astype(BF)
    first_top[...] = ascend(tops, 0, own_up[896:960, :], near_up[896:960, :])


def lifted(own, near, top_transfer):
    return pl.pallas_call(
        lift_kernel,
        in_specs=[VMEM_SPEC] * 2 + [HBM_SPEC],
        out_specs=[VMEM_SPEC] * 4,
        out_shape=[
            pltpu.VMEM((960, PROBES), BF),
            pltpu.VMEM((960, PROBES), BF),
            pltpu.VMEM((128, 512), BF),
            pltpu.VMEM((RANK, PROBES), BF),
        ],
        scratch_shapes=[pltpu.VMEM((62, 4096), BF), pltpu.SemaphoreType.DMA],
        compiler_params=limit(6),
        name="lifted",
    )(on_chip(own), on_chip(near), off_chip(top_transfer))


def climb(tops, number, mine, first, second, third):
    def climb_kernel(tops_ref, mine_ref, first_ref, second_ref, third_ref, low_ref, high_ref):
        low = ascend(tops_ref, number, mine_ref[...], first_ref[...])
        side = ascend(tops_ref, number + 1, second_ref[...], third_ref[...])
        low_ref[...] = low
        high_ref[...] = ascend(tops_ref, number + 2, low, side)

    operands = [on_chip(x) for x in (tops, mine, first, second, third)]
    return pl.pallas_call(
        climb_kernel,
        in_specs=[VMEM_SPEC] * 5,
        out_specs=[VMEM_SPEC] * 2,
        out_shape=[pltpu.VMEM((RANK, PROBES), BF)] * 2,
        compiler_params=limit(4),
        name="climb_%d" % number,
    )(*operands)


CHUNK = 96


def place_kernel(sources, tiles_hbm, tail_ref, d0, d1, d2, d3, d4, tiles_ref, spread, sems):
    copies = []
    for k in range(11):
        size = CHUNK if k < 10 else 48
        rows = pl.ds(CHUNK * k, size)
        copies.append(pltpu.make_async_copy(tiles_hbm.at[rows], tiles_ref.at[rows], sems.at[k]))
        copies[-1].start()
    device = lax.axis_index("leaf")
    odd = device & 1

    def slot_of(entry, height):
        shift = 4 - height
        index = sources[entry] - ((device - 2) << shift)
        piece = index >> shift
        piece = jnp.where(odd == 1, 4 - piece, piece)
        piece = jnp.where(
            piece == 2,
            0,
            jnp.where(piece == 3, 1, jnp.where(piece == 4, 2, jnp.where(piece == 1, 3, 4))),
        )
        return (piece << shift) + (index & ((1 << shift) - 1))

    order = group_order()
    eye = identity(128)

    def scatter(first_row, entries):
        for row in range(0, len(entries), 16):
            at = first_row + row
            if not isinstance(at, int):
                at = pl.multiple_of(at, 16)
            if len(entries) - row < 16:
                block = jnp.concatenate([tail_ref[...], jnp.zeros((1, 4096), BF)], axis=0)
            else:
                block = tiles_ref[pl.ds(at, 16), :]
            regroup = regrouped(block, order)
            for e in range(min(16, len(entries) - row)):
                base, height, entry = entries[row + e]
                at = base + slot_of(entry, height)
                spread[at, 0:16, :] = regroup[16 * e : 16 * e + 16, :128]
                spread[at, 16:32, :] = regroup[16 * e : 16 * e + 16, 128:]

    def emit(out, base, count, row):
        for piece in range(5):
            at = base + piece * count
            flat = spread[at : at + count].reshape(count * HALF, 128)
            flip = dot_nt(eye, flat).astype(BF)
            width = count * HALF
            out[piece, pl.ds(row, RANK), 0:width] = flip[:RANK]
            out[piece, pl.ds(row, RANK), width : 2 * width] = flip[RANK:]

    def clear():
        spread[...] = jnp.zeros_like(spread)

    def leaves(k, carry):
        pltpu.make_async_copy(tiles_hbm.at[pl.ds(0, CHUNK)], tiles_ref.at[pl.ds(0, CHUNK)], sems.at[k]).wait()
        base = k * CHUNK
        clear()
        scatter(base, [(80 * (e // 48), 0, base + e) for e in range(CHUNK)])
        for t in range(2):
            emit(d0, 80 * t, 16, pl.multiple_of(k * 128 + RANK * t, RANK))
        return carry

    lax.fori_loop(0, 8, leaves, 0)
    for k in range(8, 10):
        copies[k].wait()
        base = k * CHUNK
        clear()
        scatter(base, [(40 * (e // 24), 1, base + e) for e in range(CHUNK)])
        for t in range(4):
            emit(d1, 40 * t, 8, (k - 8) * 256 + RANK * t)
    copies[10].wait()
    clear()
    entries = [(20 * (e // 12), 2, 960 + e) for e in range(48)]
    entries += [(80 + 10 * (e // 6), 3, 1008 + e) for e in range(12)]
    entries += [(100, 4, 1020 + e) for e in range(3)]
    scatter(960, entries)
    for t in range(4):
        emit(d2, 20 * t, 4, RANK * t)
    for t in range(2):
        emit(d3, 80 + 10 * t, 2, RANK * t)
    emit(d4, 100, 1, 0)


def placed_tiles(sources, couplings):
    return pl.pallas_call(
        place_kernel,
        in_specs=[pl.BlockSpec(memory_space=pltpu.SMEM), HBM_SPEC, VMEM_SPEC],
        out_specs=[VMEM_SPEC] * 5,
        out_shape=[pltpu.VMEM((5, RANK * c, RANK * c), BF) for c in COUNTS],
        scratch_shapes=[
            pltpu.VMEM((1008, 4096), BF),
            pltpu.VMEM((160, HALF, 128), BF),
            pltpu.SemaphoreType.DMA((11,)),
        ],
        compiler_params=limit(14),
        name="placed_tiles",
    )(sources, off_chip(couplings), on_chip(couplings[1008:]))


ROWS = (0, 512, 768, 896)


def iotas(rows, columns):
    shape = (rows, columns)
    return (
        lax.broadcasted_iota(jnp.int32, shape, 0),
        lax.broadcasted_iota(jnp.int32, shape, 1),
    )


def natural(rank):
    return (rank & 31) * 2 + (rank >> 5)


def ones_where(mask):
    return jnp.where(mask, 1.0, 0.0).astype(BF)


def rank_order():
    row, column = iotas(RANK, RANK)
    return ones_where(column == natural(row))


def rank_order_pair():
    row, column = iotas(2 * RANK, 2 * RANK)
    return ones_where(column == (row & 64) + natural(row & 63))


def identity(size):
    row, column = iotas(size, size)
    return ones_where(row == column)


def group_order():
    row, column = iotas(256, 256)
    return ones_where(column == (row & 15) * 16 + (row >> 4))


def dot(left, right):
    return jnp.dot(left, right, preferred_element_type=F32)


def dot_nt(left, right):
    return lax.dot_general(left, right, (((1,), (1,)), ((), ())), preferred_element_type=F32)


def regrouped(block, order):
    halves = [
        jnp.concatenate(
            [block[:, (16 * half + g) * 128 : (16 * half + g + 1) * 128] for g in range(16)], axis=0
        )
        for half in range(2)
    ]
    return dot(order, jnp.concatenate(halves, axis=1)).astype(BF)


def tile_rows(regroup):
    pieces = []
    for entry in range(16):
        rows = slice(16 * entry, 16 * entry + 16)
        pieces.append(regroup[rows, :128])
        pieces.append(regroup[rows, 128:])
    return jnp.concatenate(pieces, axis=0)


def first_kernel(points_hbm, basis_hbm, links_hbm, out_ref, points_ref, basis_ref, links_ref, sems):
    links_copy = pltpu.make_async_copy(links_hbm, links_ref, sems.at[9])
    links_copy.start()
    basis_copy = pltpu.make_async_copy(basis_hbm, basis_ref, sems.at[8])
    basis_copy.start()
    copies = []
    for k in range(8):
        rows = pl.ds(512 * k, 512)
        copies.append(pltpu.make_async_copy(points_hbm.at[rows], points_ref.at[rows], sems.at[k]))
        copies[-1].start()
    order = group_order()
    flip = rank_order_pair()
    ranks = rank_order()
    links_copy.wait()
    high = jnp.concatenate([links_ref[16:30, :], jnp.zeros((2, 4096), BF)], axis=0)
    for number, block in enumerate((links_ref[0:16, :], high)):
        tiles = tile_rows(regrouped(block, order))
        out_ref[1024 + 128 * number : 1152 + 128 * number, :] = dot_nt(flip, tiles).astype(BF)
    basis_copy.wait()
    for k in range(8):
        basis = jnp.concatenate([basis_ref[2 * k], basis_ref[2 * k + 1]], axis=1)
        basis = dot(ranks, basis).astype(BF)
        copies[k].wait()
        for j in range(2):
            at = 512 * k + LEAF * j
            moment = dot(basis[:, LEAF * j : LEAF * (j + 1)], points_ref[at : at + LEAF, :]).astype(BF)
            to = (2 * k + j) * HALF
            out_ref[to : to + HALF, :] = moment[:HALF]
            out_ref[512 + to : 512 + to + HALF, :] = moment[HALF:]


VMEM_SPEC = pl.BlockSpec(memory_space=pltpu.VMEM)
HBM_SPEC = pl.BlockSpec(memory_space=pl.ANY)


def on_chip(value):
    return pltpu.with_memory_space_constraint(value, pltpu.VMEM)


def off_chip(value):
    return pltpu.with_memory_space_constraint(value, pltpu.HBM)


def limit(mebibytes):
    return pltpu.CompilerParams(vmem_limit_bytes=mebibytes << 20)


def first_moments(points, leaf_basis, local_transfer):
    return pl.pallas_call(
        first_kernel,
        in_specs=[HBM_SPEC] * 3,
        out_specs=VMEM_SPEC,
        out_shape=pltpu.VMEM((1280, PROBES), BF),
        scratch_shapes=[
            pltpu.VMEM((4096, PROBES), BF),
            pltpu.VMEM((LEAF_DEV, RANK, LEAF), BF),
            pltpu.VMEM((30, 4096), BF),
            pltpu.SemaphoreType.DMA((10,)),
        ],
        compiler_params=limit(10),
        name="first_moments",
    )(off_chip(points), off_chip(leaf_basis), off_chip(local_transfer))


def lift_into(packet, upper):
    low_side = lax.broadcasted_iota(jnp.int32, (RANK, 128), 1) < 64
    zero = jnp.zeros((RANK, 128), BF)

    def pair_of_targets(links, lanes, source, start, stride):
        total = None
        for side in range(2):
            left = packet[links + RANK * side : links + RANK * (side + 1), lanes : lanes + 128]
            left = jnp.concatenate(
                [jnp.where(low_side, left, zero), jnp.where(low_side, zero, left)], axis=0
            )
            begin = start + stride * side
            product = dot(left, source[begin : begin + 128, :])
            total = product if total is None else total + product
        return total.astype(BF)

    def keep(moment, base, count, first):
        for j in range(2):
            for side in range(2):
                at = base + side * count * HALF + (first + j) * HALF
                upper[at : at + HALF, :] = moment[j * RANK + side * HALF : j * RANK + (side + 1) * HALF]

    for u in range(4):
        keep(pair_of_targets(1024, 128 * u, packet, 128 * u, 512), 0, 8, 2 * u)
    for u in range(2):
        keep(pair_of_targets(1152, 128 * u, upper, 128 * u, 256), 512, 4, 2 * u)
    keep(pair_of_targets(1152, 256, upper, 512, 128), 768, 2, 0)
    total = None
    for side in range(2):
        left = packet[1152 + RANK * side : 1152 + RANK * (side + 1), 384:448]
        product = dot(left, upper[768 + 64 * side : 768 + 64 * side + 64, :])
        total = product if total is None else total + product
    upper[896:960, :] = total.astype(BF)


def ascend(tops, number, mine, other):
    total = None
    for side in range(2):
        left = tops[RANK * side : RANK * (side + 1), 64 * number : 64 * number + 64]
        rows = slice(HALF * side, HALF * (side + 1))
        product = dot(left, jnp.concatenate([mine[rows], other[rows]], axis=0))
        total = product if total is None else total + product
    return total.astype(BF)


PICKS = (
    (0, 0, 0), (0, 0, 1),
    (32, 1, 0), (32, 1, 1), (32, 1, 2), (32, 1, 3),
    (48, 2, 0), (48, 2, 1),
    (56, 3, 0), (56, 3, 1), (56, 3, 2), (56, 3, 3),
    (60, 4, 0), (60, 4, 1),
)


def lift_kernel(own, near, top_hbm, own_up, near_up, tops, first_top, top_ref, sem):
    copy = pltpu.make_async_copy(top_hbm, top_ref, sem)
    copy.start()
    lift_into(own, own_up)
    lift_into(near, near_up)
    device = lax.axis_index("leaf")
    row, column = iotas(16, 62)
    chosen = jnp.full((16, 62), -1, jnp.int32)
    for number, (begin, shift, flip) in enumerate(PICKS):
        chosen = jnp.where(row == number, begin + ((device >> shift) ^ flip), chosen)
    pick = ones_where(column == chosen)
    copy.wait()
    rows = dot(pick, top_ref[...]).astype(BF)
    tops[...] = dot_nt(rank_order_pair(), tile_rows(regrouped(rows, group_order()))).astype(BF)
    first_top[...] = ascend(tops, 0, own_up[896:960, :], near_up[896:960, :])


def lifted(own, near, top_transfer):
    return pl.pallas_call(
        lift_kernel,
        in_specs=[VMEM_SPEC] * 2 + [HBM_SPEC],
        out_specs=[VMEM_SPEC] * 4,
        out_shape=[
            pltpu.VMEM((960, PROBES), BF),
            pltpu.VMEM((960, PROBES), BF),
            pltpu.VMEM((128, 512), BF),
            pltpu.VMEM((RANK, PROBES), BF),
        ],
        scratch_shapes=[pltpu.VMEM((62, 4096), BF), pltpu.SemaphoreType.DMA],
        compiler_params=limit(6),
        name="lifted",
    )(on_chip(own), on_chip(near), off_chip(top_transfer))


def climb(tops, number, mine, first, second, third):
    def climb_kernel(tops_ref, mine_ref, first_ref, second_ref, third_ref, low_ref, high_ref):
        low = ascend(tops_ref, number, mine_ref[...], first_ref[...])
        side = ascend(tops_ref, number + 1, second_ref[...], third_ref[...])
        low_ref[...] = low
        high_ref[...] = ascend(tops_ref, number + 2, low, side)

    operands = [on_chip(x) for x in (tops, mine, first, second, third)]
    return pl.pallas_call(
        climb_kernel,
        in_specs=[VMEM_SPEC] * 5,
        out_specs=[VMEM_SPEC] * 2,
        out_shape=[pltpu.VMEM((RANK, PROBES), BF)] * 2,
        compiler_params=limit(4),
        name="climb_%d" % number,
    )(*operands)


def place_kernel(sources, tiles_ref, d0, d1, d2, d3, d4, spread):
    step = pl.program_id(0)
    device = lax.axis_index("leaf")
    odd = device & 1

    def slot_of(entry, height):
        shift = 4 - height
        index = sources[entry] - ((device - 2) << shift)
        piece = index >> shift
        piece = jnp.where(odd == 1, 4 - piece, piece)
        piece = jnp.where(
            piece == 2,
            0,
            jnp.where(piece == 3, 1, jnp.where(piece == 4, 2, jnp.where(piece == 1, 3, 4))),
        )
        return (piece << shift) + (index & ((1 << shift) - 1))

    order = group_order()
    eye = identity(128)

    def scatter(first_row, entries):
        row = first_row
        while row < first_row + len(entries):
            block = tiles_ref[row : row + 16, :]
            if len(entries) - (row - first_row) < 16:
                keep, _ = iotas(16, 4096)
                block = jnp.where(
                    keep < len(entries) - (row - first_row), block.astype(F32), 0.0
                ).astype(BF)
            regroup = regrouped(block, order)
            for e in range(min(16, len(entries) - (row - first_row))):
                base, height, entry = entries[row - first_row + e]
                at = base + slot_of(entry, height)
                spread[at, 0:16, :] = regroup[16 * e : 16 * e + 16, :128]
                spread[at, 16:32, :] = regroup[16 * e : 16 * e + 16, 128:]
            row += 16

    def flipped(base, count):
        flat = spread[base : base + count].reshape(count * HALF, 128)
        return dot_nt(eye, flat).astype(BF)

    def emit(out, base, count, row):
        for piece in range(5):
            flip = flipped(base + piece * count, count)
            width = count * HALF
            out[piece, row : row + RANK, 0:width] = flip[:RANK]
            out[piece, row : row + RANK, width : 2 * width] = flip[RANK:]

    spread[...] = jnp.zeros_like(spread)

    @pl.when(step < 8)
    def _():
        base = step * 96
        scatter(0, [(80 * (e // 48), 0, base + e) for e in range(96)])
        for t in range(2):
            emit(d0, 80 * t, 16, RANK * t)

    @pl.when((step >= 8) & (step < 10))
    def _():
        base = step * 96
        scatter(0, [(40 * (e // 24), 1, base + e) for e in range(96)])
        for t in range(4):
            emit(d1, 40 * t, 8, RANK * t)

    @pl.when(step == 10)
    def _():
        entries = [(20 * (e // 12), 2, 960 + e) for e in range(48)]
        entries += [(80 + 10 * (e // 6), 3, 1008 + e) for e in range(12)]
        entries += [(100, 4, 1020 + e) for e in range(3)]
        scatter(0, entries)
        for t in range(4):
            emit(d2, 20 * t, 4, RANK * t)
        for t in range(2):
            emit(d3, 80 + 10 * t, 2, RANK * t)
        emit(d4, 100, 1, 0)


def placed_tiles(sources, couplings):
    return pl.pallas_call(
        place_kernel,
        grid_spec=pltpu.PrefetchScalarGridSpec(
            num_scalar_prefetch=1,
            grid=(11,),
            in_specs=[pl.BlockSpec((96, 4096), lambda i, s: (i, 0))],
            out_specs=[
                pl.BlockSpec((5, 128, 1024), lambda i, s: (0, jnp.minimum(i, 7), 0)),
                pl.BlockSpec((5, 256, 512), lambda i, s: (0, jnp.clip(i - 8, 0, 1), 0)),
                pl.BlockSpec((5, 256, 256), lambda i, s: (0, 0, 0)),
                pl.BlockSpec((5, 128, 128), lambda i, s: (0, 0, 0)),
                pl.BlockSpec((5, 64, 64), lambda i, s: (0, 0, 0)),
            ],
            scratch_shapes=[pltpu.VMEM((160, HALF, 128), BF)],
        ),
        out_shape=[
            jax.ShapeDtypeStruct((5, RANK * c, RANK * c), BF) for c in COUNTS
        ],
        name="placed_tiles",
    )(sources, couplings)


ROWS = (0, 1024, 1536, 1792, 1920)


def couple_pieces(total, pieces, dense):
    for height, count in enumerate(COUNTS):
        width = RANK * count
        value = total(height)
        for packet, upper, tile in pieces:
            if height == 0:
                moment = packet[0:1024, :]
            else:
                at = LIFT_ROWS[height - 1]
                moment = upper[at : at + width, :]
            product = dot(dense[height][tile], moment)
            value = product if value is None else value + product
        yield height, width, value


def near_kernel(own, near, own_up, near_up, d0, d1, d2, d3, d4, out):
    pieces = ((own, own_up, 0), (near, near_up, 1))
    for height, width, value in couple_pieces(lambda h: None, pieces, (d0, d1, d2, d3, d4)):
        out[ROWS[height] : ROWS[height] + width, :] = value


def far_kernel(first, second, third, acc, t1, t2, t3, t4, t5, d0, d1, d2, d3, d4, out, tops, up_a, up_b, up_c):
    row, column = iotas(RANK, RANK)
    back = ones_where(natural(column) == row)
    for k, top in enumerate((t1, t2, t3, t4, t5)):
        tops[k] = dot(back, top[...]).astype(BF)
    lift_into(first, up_a)
    lift_into(second, up_b)
    lift_into(third, up_c)
    pieces = ((first, up_a, 2), (second, up_b, 4), (third, up_c, 3))
    start = lambda h: acc[ROWS[h] : ROWS[h] + RANK * COUNTS[h], :]
    for height, width, value in couple_pieces(start, pieces, (d0, d1, d2, d3, d4)):
        out[ROWS[height] : ROWS[height] + width, :] = value.astype(BF)


def couple_near(own, near, own_up, near_up, dense):
    operands = [on_chip(x) for x in (own, near, own_up, near_up, *dense)]
    return pl.pallas_call(
        near_kernel,
        in_specs=[VMEM_SPEC] * 9,
        out_specs=VMEM_SPEC,
        out_shape=pltpu.VMEM((1984, PROBES), F32),
        compiler_params=limit(8),
        name="couple_near",
    )(*operands)


def couple_far(first, second, third, acc, tops, dense):
    operands = [on_chip(x) for x in (first, second, third, acc, *tops, *dense)]
    return pl.pallas_call(
        far_kernel,
        in_specs=[VMEM_SPEC] * 14,
        out_specs=[VMEM_SPEC] * 2,
        out_shape=[
            jax.ShapeDtypeStruct((1984, PROBES), BF),
            jax.ShapeDtypeStruct((5, RANK, PROBES), BF),
        ],
        scratch_shapes=[pltpu.VMEM((960, PROBES), BF)] * 3,
        compiler_params=limit(16),
        name="couple_far",
    )(*operands)


def route(step):
    devices = range(lax.axis_size("leaf"))
    return [(i, step(i)) for i in devices if step(i) in devices]


def sent(block, step):
    return lax.ppermute(block, "leaf", route(step))


def shards(points, leaf_basis, local_transfer, top_transfer, sources, couplings):
    own = first_moments(points, leaf_basis, local_transfer)
    near = sent(own, lambda i: i ^ 1)
    inner = sent(own, lambda i: i + 2 if i % 2 else i - 2)
    outer = sent(own, lambda i: i - 2 if i % 2 else i + 2)
    own_up, near_up, tops, first_top = lifted(own, near, top_transfer)
    over = [sent(first_top, lambda i: i ^ k) for k in (2, 4, 6)]
    couplings, first_top = lax.optimization_barrier((couplings, first_top))
    dense = placed_tiles(sources, couplings)
    over, dense = lax.optimization_barrier((over, dense))
    second_top, third_top = climb(tops, 1, first_top, *over)
    across = [sent(third_top, lambda i: i ^ k) for k in (8, 16, 24)]
    own, third_top = lax.optimization_barrier((own, third_top))
    acc = couple_near(own, near, own_up, near_up, dense)
    inner, outer, across, acc = lax.optimization_barrier((inner, outer, across, acc))
    relayed = sent(inner, lambda i: i ^ 1)
    fourth_top, fifth_top = climb(tops, 4, third_top, *across)
    ladder = (first_top, second_top, third_top, fourth_top, fifth_top)
    coupled, ancestors = couple_far(inner, outer, relayed, acc, ladder, dense)
    return coupled.reshape(31, RANK, PROBES), ancestors[None]


def solution(mesh):
    placed = (
        P("leaf", "probe"),
        P("leaf", None, None),
        P("leaf", None),
        P(),
        P("leaf"),
        P("leaf", None),
    )
    return jax.shard_map(
        shards,
        mesh=mesh,
        in_specs=placed,
        out_specs=(P("leaf", None, "probe"), P("leaf", None, None, "probe")),
        check_vma=False,
    )
```

time: 159 us -> 77.3 us (0.49)
  the two profiles are of different devices: /device:TPU:103 before, /device:TPU:1 now
where the time goes in v1:
time: 77.3 us; the launch traced here: 76.5 us
  Pallas kernels  40.1 us (52%)
  starting transfers between devices  19.8 us (26%)
  local copies, waits for them, and re-layouts  12.9 us (17%)
  waiting for transfers between devices  2.98 us (4%)
    pallas_call x1, Pallas kernels, placed_tiles(): pl.pallas_call(place_kernel, grid_spec=pltpu.PrefetchScalarGridSpec(num_s...  20 us
    ppermute x10, starting transfers between devices, sent(): return lax.ppermute(block, 'leaf', route(step))  19.8 us
    unnamed x22, local copies, waits for them, and re-layouts  12.9 us
    pallas_call x1, Pallas kernels, couple_far(): pl.pallas_call(far_kernel, in_specs=[VMEM_SPEC] * 14, out_specs=[VMEM_SPE...  10.2 us
    pallas_call x1, Pallas kernels, first_moments(): pl.pallas_call(first_kernel, in_specs=[HBM_SPEC] * 3, out_specs=VMEM_SPEC...  3.47 us
    pallas_call x1, Pallas kernels, couple_near(): pl.pallas_call(near_kernel, in_specs=[VMEM_SPEC] * 9, out_specs=VMEM_SPEC...  3.1 us
    ppermute x10, waiting for transfers between devices, sent(): return lax.ppermute(block, 'leaf', route(step))  2.98 us
    pallas_call x1, Pallas kernels, lifted(): pl.pallas_call(lift_kernel, in_specs=[VMEM_SPEC] * 2 + [HBM_SPEC], out_sp...  2.51 us
  transfers between devices with their start and end apart: 10, of which 2 were waited for; matrix products, arithmetic and copies ran while one was open for 0% of the time, Pallas kernels for 35%

profile of v1, /device:TPU:1, one launch (start us, length us, event | category | flops | bytes accessed | tf_op | source)
XLA Modules:
  0.0 76.5 jit_solution(17573328311936745433)
XLA Ops:
  0.6 3.5 %first_moments.1.own = bf16[1280,512]{1,0:T(8,128)(2,1)S(1)} custom-call(bf16[4096,512]{1,0:T(8,128)(2,1)} %points_hbm.1, bf16[16,64,256]{2,1,0:T(8,128)(2,1)} %basis_hbm.1, bf16[30,4096]{1,0:T(8,128)(2,1)} %links_hbm.1), custom_call_target="tpu_custom_call" | custom-call | tf_op jit(solution)/shard_map/first_moments/pallas_call | solution.py:470
  4.1 1.5 %collective-permute-start.2 = (bf16[1280,512]{1,0:T(8,128)(2,1)S(1)}, bf16[1280,512]{1,0:T(8,128)(2,1)S(1)}, u32[]{:S(2)}, u32[]{:S(2)}) collective-permute-start(bf16[1280,512]{1,0:T(8,128)(2,1)S(1)} %first_moments.1.own), channel_id=1, source_target_pairs={{0,4},{4,0},{8,12},{12,8},{16,20},{20,16},{24,28},{28,24},{32,36},... | collective-permute-start | bytes 3932168 | tf_op jit(solution)/shard_map/ppermute | solution.py:764
  5.6 4.3 %collective-permute-start = (bf16[1280,512]{1,0:T(8,128)(2,1)S(1)}, bf16[1280,512]{1,0:T(8,128)(2,1)}, u32[]{:S(2)}, u32[]{:S(2)}) collective-permute-start(bf16[1280,512]{1,0:T(8,128)(2,1)S(1)} %first_moments.1.own), channel_id=1, source_target_pairs={{4,12},{8,0},{12,20},{16,8},{20,28},{24,16},{28,36},{32,24},{36,44... | collective-permute-start | bytes 3932168 | tf_op jit(solution)/shard_map/ppermute | solution.py:764
  9.9 1.3 %collective-permute-start.1 = (bf16[1280,512]{1,0:T(8,128)(2,1)S(1)}, bf16[1280,512]{1,0:T(8,128)(2,1)}, u32[]{:S(2)}, u32[]{:S(2)}) collective-permute-start(bf16[1280,512]{1,0:T(8,128)(2,1)S(1)} %first_moments.1.own), channel_id=1, source_target_pairs={{0,8},{8,16},{12,4},{16,24},{20,12},{24,32},{28,20},{32,40},{36,28... | collective-permute-start | bytes 3932168 | tf_op jit(solution)/shard_map/ppermute | solution.py:764
  11.2 2.5 %lifted.1 = (bf16[960,512]{1,0:T(8,128)(2,1)S(1)}, bf16[960,512]{1,0:T(8,128)(2,1)S(1)}, bf16[128,512]{1,0:T(8,128)(2,1)S(1)}, bf16[64,512]{1,0:T(8,128)(2,1)S(1)}) custom-call(bf16[1280,512]{1,0:T(8,128)(2,1)S(1)} %first_moments.1.own, bf16[1280,512]{1,0:T(8,128)(2,1)S(1)} %collective-permute-done.2.near, bf16[62,4096]{1,0:T(8,128)(2,1)} %top_hbm.1), custom_call_target="tpu_custom_call" | custom-call | tf_op jit(solution)/shard_map/lifted/pallas_call | solution.py:558
  13.7 0.9 %copy-done.4 = bf16[960,512]{1,0:T(8,128)(2,1)} copy-done((bf16[960,512]{1,0:T(8,128)(2,1)}, bf16[960,512]{1,0:T(8,128)(2,1)S(1)}, u32[]{:S(2)}) %copy-start.4) | copy-done | bytes 983064
  14.6 0.9 %copy-done.6 = bf16[960,512]{1,0:T(8,128)(2,1)} copy-done((bf16[960,512]{1,0:T(8,128)(2,1)}, bf16[960,512]{1,0:T(8,128)(2,1)S(1)}, u32[]{:S(2)}) %copy-start.6) | copy-done | bytes 983064
  15.6 2.1 %collective-permute-start.3 = (bf16[64,512]{1,0:T(8,128)(2,1)S(1)}, bf16[64,512]{1,0:T(8,128)(2,1)S(1)}, u32[]{:S(2)}, u32[]{:S(2)}) collective-permute-start(bf16[64,512]{1,0:T(8,128)(2,1)S(1)} %get-tuple-element.37.mine_ref.t1), channel_id=1, source_target_pairs={{0,8},{4,12},{8,0},{12,4},{16,24},{20,28},{24,16},{28,20},{32,40},... | collective-permute-start | bytes 196616 | tf_op jit(solution)/shard_map/ppermute | solution.py:764
  17.6 1.4 %collective-permute-start.4 = (bf16[64,512]{1,0:T(8,128)(2,1)S(1)}, bf16[64,512]{1,0:T(8,128)(2,1)S(1)}, u32[]{:S(2)}, u32[]{:S(2)}) collective-permute-start(bf16[64,512]{1,0:T(8,128)(2,1)S(1)} %get-tuple-element.37.mine_ref.t1), channel_id=1, source_target_pairs={{0,16},{4,20},{8,24},{12,28},{16,0},{20,4},{24,8},{28,12},{32,48},... | collective-permute-start | bytes 196616 | tf_op jit(solution)/shard_map/ppermute | solution.py:764
  19.1 1.0 %collective-permute-start.5 = (bf16[64,512]{1,0:T(8,128)(2,1)S(1)}, bf16[64,512]{1,0:T(8,128)(2,1)S(1)}, u32[]{:S(2)}, u32[]{:S(2)}) collective-permute-start(bf16[64,512]{1,0:T(8,128)(2,1)S(1)} %get-tuple-element.37.mine_ref.t1), channel_id=1, source_target_pairs={{0,24},{4,28},{8,16},{12,20},{16,8},{20,12},{24,0},{28,4},{32,56},... | collective-permute-start | bytes 196616 | tf_op jit(solution)/shard_map/ppermute | solution.py:764
  20.0 20.0 %placed_tiles.1 = (bf16[5,1024,1024]{2,1,0:T(8,128)(2,1)}, bf16[5,512,512]{2,1,0:T(8,128)(2,1)}, bf16[5,256,256]{2,1,0:T(8,128)(2,1)}, bf16[5,128,128]{2,1,0:T(8,128)(2,1)}, bf16[5,64,64]{2,1,0:T(8,128)(2,1)}) custom-call(s32[1023]{0:T(1024)} %sources.1, bf16[1023,4096]{1,0:T(8,128)(2,1)} %tiles_ref), custom_call_target="tpu_custom_call" | custom-call | tf_op jit(solution)/shard_map/placed_tiles/pallas_call | solution.py:670
  41.0 2.6 %collective-permute-start.6 = (bf16[64,512]{1,0:T(8,128)(2,1)S(1)}, bf16[64,512]{1,0:T(8,128)(2,1)S(1)}, u32[]{:S(2)}, u32[]{:S(2)}) collective-permute-start(bf16[64,512]{1,0:T(8,128)(2,1)S(1)} %get-tuple-element.60.mine_ref.t3), channel_id=1, source_target_pairs={{0,32},{4,36},{8,40},{12,44},{16,48},{20,52},{24,56},{28,60},{32,0... | collective-permute-start | bytes 196616 | tf_op jit(solution)/shard_map/ppermute | solution.py:764
  43.6 2.9 %collective-permute-start.7 = (bf16[64,512]{1,0:T(8,128)(2,1)S(1)}, bf16[64,512]{1,0:T(8,128)(2,1)S(1)}, u32[]{:S(2)}, u32[]{:S(2)}) collective-permute-start(bf16[64,512]{1,0:T(8,128)(2,1)S(1)} %get-tuple-element.60.mine_ref.t3), channel_id=1, source_target_pairs={{0,64},{4,68},{8,72},{12,76},{16,80},{20,84},{24,88},{28,92},{32,9... | collective-permute-start | bytes 196616 | tf_op jit(solution)/shard_map/ppermute | solution.py:764
  46.5 4.0 %copy-done = bf16[5,1024,1024]{2,1,0:T(8,128)(2,1)S(1)} copy-done((bf16[5,1024,1024]{2,1,0:T(8,128)(2,1)S(1)}, bf16[5,1024,1024]{2,1,0:T(8,128)(2,1)}, u32[]{:S(2)}) %copy-start) | copy-done | bytes 10485784
  50.5 1.7 %copy-done.2 = bf16[5,512,512]{2,1,0:T(8,128)(2,1)S(1)} copy-done((bf16[5,512,512]{2,1,0:T(8,128)(2,1)S(1)}, bf16[5,512,512]{2,1,0:T(8,128)(2,1)}, u32[]{:S(2)}) %copy-start.2) | copy-done | bytes 2621464
  52.3 1.1 %copy-done.3 = bf16[5,256,256]{2,1,0:T(8,128)(2,1)S(1)} copy-done((bf16[5,256,256]{2,1,0:T(8,128)(2,1)S(1)}, bf16[5,256,256]{2,1,0:T(8,128)(2,1)}, u32[]{:S(2)}) %copy-start.3) | copy-done | bytes 655384
  53.4 1.2 %copy-done.5 = bf16[960,512]{1,0:T(8,128)(2,1)S(1)} copy-done((bf16[960,512]{1,0:T(8,128)(2,1)S(1)}, bf16[960,512]{1,0:T(8,128)(2,1)}, u32[]{:S(2)}) %copy-start.5) | copy-done | bytes 983064
  54.6 1.2 %copy-done.7 = bf16[960,512]{1,0:T(8,128)(2,1)S(1)} copy-done((bf16[960,512]{1,0:T(8,128)(2,1)S(1)}, bf16[960,512]{1,0:T(8,128)(2,1)}, u32[]{:S(2)}) %copy-start.7) | copy-done | bytes 983064
  55.8 0.9 %copy-done.8 = bf16[5,128,128]{2,1,0:T(8,128)(2,1)S(1)} copy-done((bf16[5,128,128]{2,1,0:T(8,128)(2,1)S(1)}, bf16[5,128,128]{2,1,0:T(8,128)(2,1)}, u32[]{:S(2)}) %copy-start.8) | copy-done | bytes 163864
  56.7 0.9 %copy-done.10 = bf16[5,64,64]{2,1,0:T(8,128)(2,1)S(1)} copy-done((bf16[5,64,64]{2,1,0:T(8,128)(2,1)S(1)}, bf16[5,64,64]{2,1,0:T(8,128)(2,1)}, u32[]{:S(2)}) %copy-start.10) | copy-done | bytes 40984
  57.6 3.1 %couple_near.1.acc = f32[1984,512]{1,0:T(8,128)S(1)} custom-call(bf16[1280,512]{1,0:T(8,128)(2,1)S(1)} %first_moments.1.own, bf16[1280,512]{1,0:T(8,128)(2,1)S(1)} %collective-permute-done.2.near, bf16[960,512]{1,0:T(8,128)(2,1)S(1)} %copy-done.5, bf16[960,512]{1,0:T(8,128)(2,1)S(1)} %copy-done.7, bf16[5,1024,1024]{2,1,0:T(8,128)(2,1)S(1)} %copy-done, ...), custom_call_target="tpu_custom_call" | custom-call | tf_op jit(solution)/shard_map/couple_near/pallas_call | solution.py:732
  60.7 2.7 %collective-permute-start.9 = (bf16[1280,512]{1,0:T(8,128)(2,1)}, bf16[1280,512]{1,0:T(8,128)(2,1)S(1)}, u32[]{:S(2)}, u32[]{:S(2)}) collective-permute-start(bf16[1280,512]{1,0:T(8,128)(2,1)} %collective-permute-done.first), channel_id=1, source_target_pairs={{0,4},{4,0},{8,12},{12,8},{16,20},{20,16},{24,28},{28,24},{32,36},... | collective-permute-start | bytes 3932168 | tf_op jit(solution)/shard_map/ppermute | solution.py:764
  63.8 2.5 %collective-permute-done.9.third = bf16[1280,512]{1,0:T(8,128)(2,1)S(1)} collective-permute-done((bf16[1280,512]{1,0:T(8,128)(2,1)}, bf16[1280,512]{1,0:T(8,128)(2,1)S(1)}, u32[]{:S(2)}, u32[]{:S(2)}) %collective-permute-start.9) | collective-permute-done | bytes 1310752 | tf_op jit(solution)/shard_map/ppermute | solution.py:764
  66.3 10.2 %couple_far.1 = (bf16[1984,512]{1,0:T(8,128)(2,1)}, bf16[5,64,512]{2,1,0:T(8,128)(2,1)}) custom-call(bf16[1280,512]{1,0:T(8,128)(2,1)} %collective-permute-done.first, bf16[1280,512]{1,0:T(8,128)(2,1)} %collective-permute-done.1.second, bf16[1280,512]{1,0:T(8,128)(2,1)S(1)} %collective-permute-done.9.third, f32[1984,512]{1,0:T(8,128)S(1)} %couple_near.1.acc, ...), custom_call_target="tpu_custom_call" | custom-call | tf_op jit(solution)/shard_map/couple_far/pallas_call | solution.py:744
  (25 shorter events, 1.3 us)
Async XLA Ops:
  4.1 7.0 %collective-permute-start.2 = (bf16[1280,512]{1,0:T(8,128)(2,1)S(1)}, bf16[1280,512]{1,0:T(8,128)(2,1)S(1)}, u32[]{:S(2)}, u32[]{:S(2)}) collective-permute-start(bf16[1280,512]{1,0:T(8,128)(2,1)S(1)} %first_moments.1.own), channel_id=1, source_target_pairs={{0,4},{4,0},{8,12},{12,8},{16,20},{20,16},{24,28},{28,24},{32,36},... | collective-permute-start | bytes 3932168 | tf_op jit(solution)/shard_map/ppermute | solution.py:764
  5.6 55.1 %collective-permute-start = (bf16[1280,512]{1,0:T(8,128)(2,1)S(1)}, bf16[1280,512]{1,0:T(8,128)(2,1)}, u32[]{:S(2)}, u32[]{:S(2)}) collective-permute-start(bf16[1280,512]{1,0:T(8,128)(2,1)S(1)} %first_moments.1.own), channel_id=1, source_target_pairs={{4,12},{8,0},{12,20},{16,8},{20,28},{24,16},{28,36},{32,24},{36,44... | collective-permute-start | bytes 3932168 | tf_op jit(solution)/shard_map/ppermute | solution.py:764
  9.9 50.8 %collective-permute-start.1 = (bf16[1280,512]{1,0:T(8,128)(2,1)S(1)}, bf16[1280,512]{1,0:T(8,128)(2,1)}, u32[]{:S(2)}, u32[]{:S(2)}) collective-permute-start(bf16[1280,512]{1,0:T(8,128)(2,1)S(1)} %first_moments.1.own), channel_id=1, source_target_pairs={{0,8},{8,16},{12,4},{16,24},{20,12},{24,32},{28,20},{32,40},{36,28... | collective-permute-start | bytes 3932168 | tf_op jit(solution)/shard_map/ppermute | solution.py:764
  13.7 0.9 %copy-start.4 = (bf16[960,512]{1,0:T(8,128)(2,1)}, bf16[960,512]{1,0:T(8,128)(2,1)S(1)}, u32[]{:S(2)}) copy-start(bf16[960,512]{1,0:T(8,128)(2,1)S(1)} %get-tuple-element.49.own_up) | copy-start | bytes 2949124
  14.6 0.9 %copy-start.6 = (bf16[960,512]{1,0:T(8,128)(2,1)}, bf16[960,512]{1,0:T(8,128)(2,1)S(1)}, u32[]{:S(2)}) copy-start(bf16[960,512]{1,0:T(8,128)(2,1)S(1)} %get-tuple-element.50.near_up) | copy-start | bytes 2949124
  15.6 25.0 %collective-permute-start.3 = (bf16[64,512]{1,0:T(8,128)(2,1)S(1)}, bf16[64,512]{1,0:T(8,128)(2,1)S(1)}, u32[]{:S(2)}, u32[]{:S(2)}) collective-permute-start(bf16[64,512]{1,0:T(8,128)(2,1)S(1)} %get-tuple-element.37.mine_ref.t1), channel_id=1, source_target_pairs={{0,8},{4,12},{8,0},{12,4},{16,24},{20,28},{24,16},{28,20},{32,40},... | collective-permute-start | bytes 196616 | tf_op jit(solution)/shard_map/ppermute | solution.py:764
  17.6 22.9 %collective-permute-start.4 = (bf16[64,512]{1,0:T(8,128)(2,1)S(1)}, bf16[64,512]{1,0:T(8,128)(2,1)S(1)}, u32[]{:S(2)}, u32[]{:S(2)}) collective-permute-start(bf16[64,512]{1,0:T(8,128)(2,1)S(1)} %get-tuple-element.37.mine_ref.t1), channel_id=1, source_target_pairs={{0,16},{4,20},{8,24},{12,28},{16,0},{20,4},{24,8},{28,12},{32,48},... | collective-permute-start | bytes 196616 | tf_op jit(solution)/shard_map/ppermute | solution.py:764
  19.1 21.5 %collective-permute-start.5 = (bf16[64,512]{1,0:T(8,128)(2,1)S(1)}, bf16[64,512]{1,0:T(8,128)(2,1)S(1)}, u32[]{:S(2)}, u32[]{:S(2)}) collective-permute-start(bf16[64,512]{1,0:T(8,128)(2,1)S(1)} %get-tuple-element.37.mine_ref.t1), channel_id=1, source_target_pairs={{0,24},{4,28},{8,16},{12,20},{16,8},{20,12},{24,0},{28,4},{32,56},... | collective-permute-start | bytes 196616 | tf_op jit(solution)/shard_map/ppermute | solution.py:764
  41.0 19.7 %collective-permute-start.6 = (bf16[64,512]{1,0:T(8,128)(2,1)S(1)}, bf16[64,512]{1,0:T(8,128)(2,1)S(1)}, u32[]{:S(2)}, u32[]{:S(2)}) collective-permute-start(bf16[64,512]{1,0:T(8,128)(2,1)S(1)} %get-tuple-element.60.mine_ref.t3), channel_id=1, source_target_pairs={{0,32},{4,36},{8,40},{12,44},{16,48},{20,52},{24,56},{28,60},{32,0... | collective-permute-start | bytes 196616 | tf_op jit(solution)/shard_map/ppermute | solution.py:764
  43.6 17.1 %collective-permute-start.7 = (bf16[64,512]{1,0:T(8,128)(2,1)S(1)}, bf16[64,512]{1,0:T(8,128)(2,1)S(1)}, u32[]{:S(2)}, u32[]{:S(2)}) collective-permute-start(bf16[64,512]{1,0:T(8,128)(2,1)S(1)} %get-tuple-element.60.mine_ref.t3), channel_id=1, source_target_pairs={{0,64},{4,68},{8,72},{12,76},{16,80},{20,84},{24,88},{28,92},{32,9... | collective-permute-start | bytes 196616 | tf_op jit(solution)/shard_map/ppermute | solution.py:764
  46.5 14.2 %collective-permute-start.8 = (bf16[64,512]{1,0:T(8,128)(2,1)S(1)}, bf16[64,512]{1,0:T(8,128)(2,1)S(1)}, u32[]{:S(2)}, u32[]{:S(2)}) collective-permute-start(bf16[64,512]{1,0:T(8,128)(2,1)S(1)} %get-tuple-element.60.mine_ref.t3), channel_id=1, source_target_pairs={{0,96},{4,100},{8,104},{12,108},{16,112},{20,116},{24,120},{28,124... | collective-permute-start | bytes 196616 | tf_op jit(solution)/shard_map/ppermute | solution.py:764
  46.5 4.0 %copy-start = (bf16[5,1024,1024]{2,1,0:T(8,128)(2,1)S(1)}, bf16[5,1024,1024]{2,1,0:T(8,128)(2,1)}, u32[]{:S(2)}) copy-start(bf16[5,1024,1024]{2,1,0:T(8,128)(2,1)} %get-tuple-element.51.d0) | copy-start | bytes 31457284
  50.5 1.7 %copy-start.2 = (bf16[5,512,512]{2,1,0:T(8,128)(2,1)S(1)}, bf16[5,512,512]{2,1,0:T(8,128)(2,1)}, u32[]{:S(2)}) copy-start(bf16[5,512,512]{2,1,0:T(8,128)(2,1)} %get-tuple-element.52.d1) | copy-start | bytes 7864324
  52.3 1.1 %copy-start.3 = (bf16[5,256,256]{2,1,0:T(8,128)(2,1)S(1)}, bf16[5,256,256]{2,1,0:T(8,128)(2,1)}, u32[]{:S(2)}) copy-start(bf16[5,256,256]{2,1,0:T(8,128)(2,1)} %get-tuple-element.53.d2) | copy-start | bytes 1966084
  53.4 1.2 %copy-start.5 = (bf16[960,512]{1,0:T(8,128)(2,1)S(1)}, bf16[960,512]{1,0:T(8,128)(2,1)}, u32[]{:S(2)}) copy-start(bf16[960,512]{1,0:T(8,128)(2,1)} %copy-done.4) | copy-start | bytes 2949124
  54.6 1.2 %copy-start.7 = (bf16[960,512]{1,0:T(8,128)(2,1)S(1)}, bf16[960,512]{1,0:T(8,128)(2,1)}, u32[]{:S(2)}) copy-start(bf16[960,512]{1,0:T(8,128)(2,1)} %copy-done.6) | copy-start | bytes 2949124
  55.8 0.9 %copy-start.8 = (bf16[5,128,128]{2,1,0:T(8,128)(2,1)S(1)}, bf16[5,128,128]{2,1,0:T(8,128)(2,1)}, u32[]{:S(2)}) copy-start(bf16[5,128,128]{2,1,0:T(8,128)(2,1)} %get-tuple-element.54.d3) | copy-start | bytes 491524
  56.7 0.9 %copy-start.10 = (bf16[5,64,64]{2,1,0:T(8,128)(2,1)S(1)}, bf16[5,64,64]{2,1,0:T(8,128)(2,1)}, u32[]{:S(2)}) copy-start(bf16[5,64,64]{2,1,0:T(8,128)(2,1)} %get-tuple-element.55.d4) | copy-start | bytes 122884
  57.6 8.7 %copy-start.1 = (bf16[5,1024,1024]{2,1,0:T(8,128)(2,1)S(1)}, bf16[5,1024,1024]{2,1,0:T(8,128)(2,1)}, u32[]{:S(2)}) copy-start(bf16[5,1024,1024]{2,1,0:T(8,128)(2,1)} %get-tuple-element.51.d0) | copy-start | bytes 31457284
  57.6 8.7 %copy-start.9 = (bf16[5,128,128]{2,1,0:T(8,128)(2,1)S(1)}, bf16[5,128,128]{2,1,0:T(8,128)(2,1)}, u32[]{:S(2)}) copy-start(bf16[5,128,128]{2,1,0:T(8,128)(2,1)} %get-tuple-element.54.d3) | copy-start | bytes 491524
  60.7 5.6 %collective-permute-start.9 = (bf16[1280,512]{1,0:T(8,128)(2,1)}, bf16[1280,512]{1,0:T(8,128)(2,1)S(1)}, u32[]{:S(2)}, u32[]{:S(2)}) collective-permute-start(bf16[1280,512]{1,0:T(8,128)(2,1)} %collective-permute-done.first), channel_id=1, source_target_pairs={{0,4},{4,0},{8,12},{12,8},{16,20},{20,16},{24,28},{28,24},{32,36},... | collective-permute-start | bytes 3932168 | tf_op jit(solution)/shard_map/ppermute | solution.py:764

commit v2 on v0

v2 whole, which is shorter than its diff:
```python
import functools

import jax
import jax.numpy as jnp
from jax import lax
from jax.experimental import pallas as pl
from jax.experimental.pallas import tpu as pltpu
from jax.sharding import PartitionSpec as P


LEAF = 256
RANK = 64
PROBES = 512
LOCAL = 5
LEAF_DEV = 16
HALF = 32
BF = jnp.bfloat16
F32 = jnp.float32
COUNTS = (16, 8, 4, 2, 1)
LIFT_ROWS = (0, 512, 768, 896)


def iotas(rows, columns):
    shape = (rows, columns)
    return (
        lax.broadcasted_iota(jnp.int32, shape, 0),
        lax.broadcasted_iota(jnp.int32, shape, 1),
    )


def natural(rank):
    return (rank & 31) * 2 + (rank >> 5)


def ones_where(mask):
    return jnp.where(mask, 1.0, 0.0).astype(BF)


def rank_order():
    row, column = iotas(RANK, RANK)
    return ones_where(column == natural(row))


def rank_order_pair():
    row, column = iotas(2 * RANK, 2 * RANK)
    return ones_where(column == (row & 64) + natural(row & 63))


def group_order():
    row, column = iotas(256, 256)
    return ones_where(column == (row & 15) * 16 + (row >> 4))


def dot(left, right):
    return jnp.dot(left, right, preferred_element_type=F32)


def dot_nt(left, right):
    return lax.dot_general(left, right, (((1,), (1,)), ((), ())), preferred_element_type=F32)


def regrouped(block, order):
    halves = [
        jnp.concatenate(
            [block[:, (16 * half + g) * 128 : (16 * half + g + 1) * 128] for g in range(16)], axis=0
        )
        for half in range(2)
    ]
    return dot(order, jnp.concatenate(halves, axis=1)).astype(BF)


def tile_rows(regroup):
    pieces = []
    for entry in range(16):
        rows = slice(16 * entry, 16 * entry + 16)
        pieces.append(regroup[rows, :128])
        pieces.append(regroup[rows, 128:])
    return jnp.concatenate(pieces, axis=0)


def first_kernel(points_hbm, basis_hbm, links_hbm, out_ref, points_ref, basis_ref, links_ref, sems):
    links_copy = pltpu.make_async_copy(links_hbm, links_ref, sems.at[9])
    links_copy.start()
    basis_copy = pltpu.make_async_copy(basis_hbm, basis_ref, sems.at[8])
    basis_copy.start()
    copies = []
    for k in range(8):
        rows = pl.ds(512 * k, 512)
        copies.append(pltpu.make_async_copy(points_hbm.at[rows], points_ref.at[rows], sems.at[k]))
        copies[-1].start()
    order = group_order()
    flip = rank_order_pair()
    ranks = rank_order()
    links_copy.wait()
    high = jnp.concatenate([links_ref[16:30, :], jnp.zeros((2, 4096), BF)], axis=0)
    for number, block in enumerate((links_ref[0:16, :], high)):
        tiles = tile_rows(regrouped(block, order))
        out_ref[1024 + 128 * number : 1152 + 128 * number, :] = dot_nt(flip, tiles).astype(BF)
    basis_copy.wait()
    for k in range(8):
        basis = jnp.concatenate([basis_ref[2 * k], basis_ref[2 * k + 1]], axis=1)
        basis = dot(ranks, basis).astype(BF)
        copies[k].wait()
        for j in range(2):
            at = 512 * k + LEAF * j
            moment = dot(basis[:, LEAF * j : LEAF * (j + 1)], points_ref[at : at + LEAF, :]).astype(BF)
            to = (2 * k + j) * HALF
            out_ref[to : to + HALF, :] = moment[:HALF]
            out_ref[512 + to : 512 + to + HALF, :] = moment[HALF:]


VMEM_SPEC = pl.BlockSpec(memory_space=pltpu.VMEM)
HBM_SPEC = pl.BlockSpec(memory_space=pl.ANY)


def on_chip(value):
    return pltpu.with_memory_space_constraint(value, pltpu.VMEM)


def off_chip(value):
    return pltpu.with_memory_space_constraint(value, pltpu.HBM)


def limit(mebibytes):
    return pltpu.CompilerParams(vmem_limit_bytes=mebibytes << 20)


def first_moments(points, leaf_basis, local_transfer):
    return pl.pallas_call(
        first_kernel,
        in_specs=[HBM_SPEC] * 3,
        out_specs=VMEM_SPEC,
        out_shape=pltpu.VMEM((1280, PROBES), BF),
        scratch_shapes=[
            pltpu.VMEM((4096, PROBES), BF),
            pltpu.VMEM((LEAF_DEV, RANK, LEAF), BF),
            pltpu.VMEM((30, 4096), BF),
            pltpu.SemaphoreType.DMA((10,)),
        ],
        compiler_params=limit(10),
        name="first_moments",
    )(off_chip(points), off_chip(leaf_basis), off_chip(local_transfer))


def lift_into(packet, upper):
    low_side = lax.broadcasted_iota(jnp.int32, (RANK, 128), 1) < 64
    zero = jnp.zeros((RANK, 128), BF)

    def pair_of_targets(links, lanes, source, start, stride):
        total = None
        for side in range(2):
            left = packet[links + RANK * side : links + RANK * (side + 1), lanes : lanes + 128]
            left = jnp.concatenate(
                [jnp.where(low_side, left, zero), jnp.where(low_side, zero, left)], axis=0
            )
            begin = start + stride * side
            product = dot(left, source[begin : begin + 128, :])
            total = product if total is None else total + product
        return total.astype(BF)

    def keep(moment, base, count, first):
        for j in range(2):
            for side in range(2):
                at = base + side * count * HALF + (first + j) * HALF
                upper[at : at + HALF, :] = moment[j * RANK + side * HALF : j * RANK + (side + 1) * HALF]

    for u in range(4):
        keep(pair_of_targets(1024, 128 * u, packet, 128 * u, 512), 0, 8, 2 * u)
    for u in range(2):
        keep(pair_of_targets(1152, 128 * u, upper, 128 * u, 256), 512, 4, 2 * u)
    keep(pair_of_targets(1152, 256, upper, 512, 128), 768, 2, 0)
    total = None
    for side in range(2):
        left = packet[1152 + RANK * side : 1152 + RANK * (side + 1), 384:448]
        product = dot(left, upper[768 + 64 * side : 768 + 64 * side + 64, :])
        total = product if total is None else total + product
    upper[896:960, :] = total.astype(BF)


def ascend(tops, number, mine, other):
    total = None
    for side in range(2):
        left = tops[RANK * side : RANK * (side + 1), 64 * number : 64 * number + 64]
        rows = slice(HALF * side, HALF * (side + 1))
        product = dot(left, jnp.concatenate([mine[rows], other[rows]], axis=0))
        total = product if total is None else total + product
    return total.astype(BF)


PICKS = (
    (0, 0, 0), (0, 0, 1),
    (32, 1, 0), (32, 1, 1), (32, 1, 2), (32, 1, 3),
    (48, 2, 0), (48, 2, 1),
    (56, 3, 0), (56, 3, 1), (56, 3, 2), (56, 3, 3),
    (60, 4, 0), (60, 4, 1),
)


def lift_kernel(own, near, top_hbm, own_up, near_up, tops, first_top, top_ref, sem):
    copy = pltpu.make_async_copy(top_hbm, top_ref, sem)
    copy.start()
    lift_into(own, own_up)
    lift_into(near, near_up)
    device = lax.axis_index("leaf")
    row, column = iotas(16, 62)
    chosen = jnp.full((16, 62), -1, jnp.int32)
    for number, (begin, shift, flip) in enumerate(PICKS):
        chosen = jnp.where(row == number, begin + ((device >> shift) ^ flip), chosen)
    pick = ones_where(column == chosen)
    copy.wait()
    rows = dot(pick, top_ref[...]).astype(BF)
    tops[...] = dot_nt(rank_order_pair(), tile_rows(regrouped(rows, group_order()))).astype(BF)
    first_top[...] = ascend(tops, 0, own_up[896:960, :], near_up[896:960, :])


def lifted(own, near, top_transfer):
    return pl.pallas_call(
        lift_kernel,
        in_specs=[VMEM_SPEC] * 2 + [HBM_SPEC],
        out_specs=[VMEM_SPEC] * 4,
        out_shape=[
            pltpu.VMEM((960, PROBES), BF),
            pltpu.VMEM((960, PROBES), BF),
            pltpu.VMEM((128, 512), BF),
            pltpu.VMEM((RANK, PROBES), BF),
        ],
        scratch_shapes=[pltpu.VMEM((62, 4096), BF), pltpu.SemaphoreType.DMA],
        compiler_params=limit(6),
        name="lifted",
    )(on_chip(own), on_chip(near), off_chip(top_transfer))


def climb(tops, number, mine, first, second, third):
    def climb_kernel(tops_ref, mine_ref, first_ref, second_ref, third_ref, low_ref, high_ref):
        low = ascend(tops_ref, number, mine_ref[...], first_ref[...])
        side = ascend(tops_ref, number + 1, second_ref[...], third_ref[...])
        low_ref[...] = low
        high_ref[...] = ascend(tops_ref, number + 2, low, side)

    operands = [on_chip(x) for x in (tops, mine, first, second, third)]
    return pl.pallas_call(
        climb_kernel,
        in_specs=[VMEM_SPEC] * 5,
        out_specs=[VMEM_SPEC] * 2,
        out_shape=[pltpu.VMEM((RANK, PROBES), BF)] * 2,
        compiler_params=limit(4),
    )(*operands)


CHUNK = 96
SPAN = (0, 11)


def chunk_size(k):
    return CHUNK if k < 10 else 48


def place_kernel(span, sources, tiles_hbm, tail_ref, *refs):
    outs, (tiles_ref, spread_a, spread_b, sems) = refs[:-4], refs[-4:]
    begin, end = span
    for k in range(begin, end):
        size = chunk_size(k)
        pltpu.make_async_copy(
            tiles_hbm.at[pl.ds(CHUNK * k, size)],
            tiles_ref.at[pl.ds(CHUNK * (k - begin), size)],
            sems.at[k - begin],
        ).start()
    device = lax.axis_index("leaf")
    anchors = [(device - 2) << (4 - height) for height in range(LOCAL)]
    order = group_order()

    def scatter(spread, first_row, entries):
        spread[...] = jnp.zeros_like(spread)
        for row in range(0, len(entries), 16):
            at = first_row - CHUNK * begin + row
            if not isinstance(at, int):
                at = pl.multiple_of(at, 16)
            if len(entries) - row < 16:
                block = jnp.where(iotas(16, 4096)[0] < 15, tail_ref[...].astype(F32), 0.0).astype(BF)
            else:
                block = tiles_ref[pl.ds(at, 16), :]
            regroup = regrouped(block, order)
            for e in range(min(16, len(entries) - row)):
                base, height = entries[row + e]
                at = sources[first_row + row + e] - anchors[height] + base
                spread[at, 0:16, :] = regroup[16 * e : 16 * e + 16, :128]
                spread[at, 16:32, :] = regroup[16 * e : 16 * e + 16, 128:]

    def emit(spread, out, base, count, row):
        for piece in range(5):
            at = base + piece * count
            flat = spread[at : at + count].reshape(count * HALF, 128)
            flip = flat.T
            width = count * HALF
            out[piece, pl.ds(row, RANK), 0:width] = flip[:RANK]
            out[piece, pl.ds(row, RANK), width : 2 * width] = flip[RANK:]

    def fill(spread, k):
        if isinstance(k, int) and k == 10:
            entries = [(20 * (e // 12), 2) for e in range(48)]
            entries += [(80 + 10 * (e // 6), 3) for e in range(12)]
            entries += [(100, 4) for _ in range(3)]
        elif isinstance(k, int) and k >= 8:
            entries = [(40 * (e // 24), 1) for e in range(CHUNK)]
        else:
            entries = [(80 * (e // 48), 0) for e in range(CHUNK)]
        rows = pl.ds(0, CHUNK if len(entries) == CHUNK else 48)
        pltpu.make_async_copy(tiles_hbm.at[rows], tiles_ref.at[rows], sems.at[k - begin]).wait()
        scatter(spread, k * CHUNK, entries)

    def drain(spread, k):
        if isinstance(k, int) and k == 10:
            for t in range(4):
                emit(spread, outs[2], 20 * t, 4, RANK * t)
            for t in range(2):
                emit(spread, outs[3], 80 + 10 * t, 2, RANK * t)
            emit(spread, outs[4], 100, 1, 0)
        elif isinstance(k, int) and k >= 8:
            for t in range(4):
                emit(spread, outs[1], 40 * t, 8, (k - 8) * 256 + RANK * t)
        else:
            for t in range(2):
                row = k * 128 + RANK * t
                emit(spread, outs[0], 80 * t, 16, row if isinstance(k, int) else pl.multiple_of(row, RANK))

    def pair(k, carry):
        fill(spread_b, 2 * k + 1)
        drain(spread_a, 2 * k)
        fill(spread_a, 2 * k + 2)
        drain(spread_b, 2 * k + 1)
        return carry

    slots = (spread_a, spread_b)
    fill(spread_a, begin)
    at = begin
    if begin == 0:
        lax.fori_loop(0, 3, pair, 0)
        at = 6
    for k in range(at, end):
        if k + 1 < end:
            fill(slots[(k + 1) % 2], k + 1)
        drain(slots[k % 2], k)


def placed_tiles(sources, couplings, span):
    counts = COUNTS
    rows = sum(chunk_size(k) for k in range(*span))
    return pl.pallas_call(
        functools.partial(place_kernel, span),
        grid=(1,),
        in_specs=[
            pl.BlockSpec(memory_space=pltpu.SMEM),
            HBM_SPEC,
            pl.BlockSpec((16, 4096), lambda i: (63, 0)),
        ],
        out_specs=[VMEM_SPEC] * len(counts),
        out_shape=[pltpu.VMEM((5, RANK * c, RANK * c), BF) for c in counts],
        scratch_shapes=[
            pltpu.VMEM((rows, 4096), BF),
            pltpu.VMEM((160, HALF, 128), BF),
            pltpu.VMEM((160, HALF, 128), BF),
            pltpu.SemaphoreType.DMA((11,)),
        ],
        compiler_params=limit(14),
        name="placed_tiles",
    )(sources, off_chip(couplings), off_chip(couplings))


ROWS = (0, 1024, 1536, 1792, 1920)


def couple_pieces(total, pieces, dense):
    for height, count in enumerate(COUNTS):
        width = RANK * count
        value = total(height)
        for packet, upper, tile in pieces:
            if height == 0:
                moment = packet[0:1024, :]
            else:
                at = LIFT_ROWS[height - 1]
                moment = upper[at : at + width, :]
            product = dot(dense[height][tile], moment)
            value = product if value is None else value + product
        yield height, width, value


def piece_of(step):
    turn = 1 - 2 * (lax.axis_index("leaf") & 1)
    return 2 + turn * step


def middle_kernel(own, near, first, third, own_up, near_up, d0, d1, d2, d3, d4, out, up_a, up_c):
    lift_into(first, up_a)
    lift_into(third, up_c)
    pieces = (
        (own, own_up, 2),
        (near, near_up, piece_of(1)),
        (first, up_a, piece_of(2)),
        (third, up_c, piece_of(-1)),
    )
    for height, width, value in couple_pieces(lambda h: None, pieces, (d0, d1, d2, d3, d4)):
        out[ROWS[height] : ROWS[height] + width, :] = value


def last_kernel(
    packet, acc, t1, t2, t3, t4, t5, d0, d1, d2, d3, d4, out_hbm, tops_hbm, out, tops, up, sems
):
    row, column = iotas(RANK, RANK)
    back = ones_where(natural(column) == row)
    for k, top in enumerate((t1, t2, t3, t4, t5)):
        tops[k] = dot(back, top[...]).astype(BF)
    copies = [pltpu.make_async_copy(tops, tops_hbm, sems.at[5])]
    copies[-1].start()
    piece = piece_of(-2)

    def leave(first, size, number):
        rows = pl.ds(first, size)
        copies.append(pltpu.make_async_copy(out.at[rows], out_hbm.at[rows], sems.at[number]))
        copies[-1].start()

    lift_into(packet, up)
    for block in range(4):
        rows = slice(256 * block, 256 * block + 256)
        product = dot(d0[piece, rows, :], packet[0:1024, :])
        out[rows, :] = (acc[rows, :] + product).astype(BF)
        leave(256 * block, 256, block)
    for height in range(1, LOCAL):
        width = RANK * COUNTS[height]
        rows = slice(ROWS[height], ROWS[height] + width)
        at = LIFT_ROWS[height - 1]
        product = dot((d1, d2, d3, d4)[height - 1][piece], up[at : at + width, :])
        out[rows, :] = (acc[rows, :] + product).astype(BF)
    leave(1024, 960, 4)
    for copy in copies:
        copy.wait()


def couple_middle(own, near, first, third, own_up, near_up, dense):
    operands = [on_chip(x) for x in (own, near, first, third, own_up, near_up, *dense)]
    return pl.pallas_call(
        middle_kernel,
        in_specs=[VMEM_SPEC] * 11,
        out_specs=VMEM_SPEC,
        out_shape=pltpu.VMEM((1984, PROBES), F32),
        scratch_shapes=[pltpu.VMEM((960, PROBES), BF)] * 2,
        compiler_params=limit(8),
        name="couple_middle",
    )(*operands)


def couple_last(packet, acc, tops, dense):
    operands = [on_chip(x) for x in (packet, acc, *tops, *dense)]
    return pl.pallas_call(
        last_kernel,
        in_specs=[VMEM_SPEC] * 12,
        out_specs=[HBM_SPEC] * 2,
        out_shape=[
            pltpu.HBM((1984, PROBES), BF),
            pltpu.HBM((5, RANK, PROBES), BF),
        ],
        scratch_shapes=[
            pltpu.VMEM((1984, PROBES), BF),
            pltpu.VMEM((5, RANK, PROBES), BF),
            pltpu.VMEM((960, PROBES), BF),
            pltpu.SemaphoreType.DMA((6,)),
        ],
        compiler_params=limit(8),
        name="couple_last",
    )(*operands)


def route(step):
    devices = range(lax.axis_size("leaf"))
    return [(i, step(i)) for i in devices if step(i) in devices]


def sent(block, step):
    return lax.ppermute(block, "leaf", route(step))


def tied(*values):
    return lax.optimization_barrier(values)


def whole(points, leaf_basis, local_transfer, top_transfer, sources, couplings):
    own = first_moments(points, leaf_basis, local_transfer)
    near = sent(own, lambda i: i ^ 1)
    inner = sent(own, lambda i: i + 2 if i % 2 else i - 2)
    own_up, near_up, tops, first_top = lifted(own, near, top_transfer)
    over = [sent(first_top, lambda i: i ^ k) for k in (2, 4, 6)]
    couplings, first_top = tied(couplings, first_top)
    dense = placed_tiles(sources, couplings, SPAN)
    late, *dense = tied(own, *dense)
    outer = sent(late, lambda i: i - 2 if i % 2 else i + 2)
    relayed = sent(inner, lambda i: i ^ 1)
    over, dense = tied(over, dense)
    second_top, third_top = climb(tops, 1, first_top, *over)
    across = [sent(third_top, lambda i: i ^ k) for k in (8, 16, 24)]
    own, relayed, third_top = tied(own, relayed, third_top)
    acc = couple_middle(own, near, inner, relayed, own_up, near_up, dense)
    outer, across, acc = tied(outer, across, acc)
    fourth_top, fifth_top = climb(tops, 4, third_top, *across)
    ladder = (first_top, second_top, third_top, fourth_top, fifth_top)
    coupled, ancestors = couple_last(outer, acc, ladder, dense)
    return coupled.reshape(31, RANK, PROBES), ancestors[None]


def solution(mesh):
    placed = (
        P("leaf", "probe"),
        P("leaf", None, None),
        P("leaf", None),
        P(),
        P("leaf"),
        P("leaf", None),
    )
    return jax.shard_map(
        whole,
        mesh=mesh,
        in_specs=placed,
        out_specs=(P("leaf", None, "probe"), P("leaf", None, None, "probe")),
        check_vma=False,
    )
```

time: 159 us -> 77.9 us (0.49)
  the two profiles are of different devices: /device:TPU:103 before, /device:TPU:0 now
where the time goes in v2:
time: 77.9 us; the launch traced here: 77.7 us
  waiting for transfers between devices  33.8 us (43%)
  Pallas kernels  27.1 us (35%)
  starting transfers between devices  15.9 us (20%)
  between operations  0.92 us (1%)
    ppermute x10, waiting for transfers between devices, sent(): return lax.ppermute(block, 'leaf', route(step))  33.8 us
    ppermute x10, starting transfers between devices, sent(): return lax.ppermute(block, 'leaf', route(step))  15.9 us
    pallas_call x1, Pallas kernels, placed_tiles(): pl.pallas_call(functools.partial(place_kernel, span), grid=(1,), in_specs...  8.95 us
    pallas_call x1, Pallas kernels, couple_middle(): pl.pallas_call(middle_kernel, in_specs=[VMEM_SPEC] * 11, out_specs=VMEM_S...  7.73 us
    pallas_call x1, Pallas kernels, couple_last(): pl.pallas_call(last_kernel, in_specs=[VMEM_SPEC] * 12, out_specs=[HBM_SPE...  3.65 us
    pallas_call x1, Pallas kernels, first_moments(): pl.pallas_call(first_kernel, in_specs=[HBM_SPEC] * 3, out_specs=VMEM_SPEC...  3.47 us
    pallas_call x1, Pallas kernels, lifted(): pl.pallas_call(lift_kernel, in_specs=[VMEM_SPEC] * 2 + [HBM_SPEC], out_sp...  2.51 us
  transfers between devices with their start and end apart: 10, of which 3 were waited for; matrix products, arithmetic and copies ran while one was open for 0% of the time, Pallas kernels for 25%

profile of v2, /device:TPU:0, one launch (start us, length us, event | category | flops | bytes accessed | tf_op | source)
XLA Modules:
  0.0 77.7 jit_solution(2303954286367438870)
XLA Ops:
  0.6 3.5 %first_moments.1.own = bf16[1280,512]{1,0:T(8,128)(2,1)S(1)} custom-call(bf16[4096,512]{1,0:T(8,128)(2,1)} %points_hbm.1, bf16[16,64,256]{2,1,0:T(8,128)(2,1)} %basis_hbm.1, bf16[30,4096]{1,0:T(8,128)(2,1)} %links_hbm.1), custom_call_target="tpu_custom_call" | custom-call | tf_op jit(solution)/shard_map/first_moments/pallas_call | solution.py:129
  4.1 0.0 copy-start
  4.1 1.3 %collective-permute-start.8 = (bf16[1280,512]{1,0:T(8,128)(2,1)S(1)}, bf16[1280,512]{1,0:T(8,128)(2,1)S(1)}, u32[]{:S(2)}, u32[]{:S(2)}) collective-permute-start(bf16[1280,512]{1,0:T(8,128)(2,1)S(1)} %first_moments.1.own), channel_id=1, source_target_pairs={{4,12},{8,0},{12,20},{16,8},{20,28},{24,16},{28,36},{32,24},{36,44... | collective-permute-start | bytes 3932168 | tf_op jit(solution)/shard_map/ppermute | solution.py:478
  5.4 1.9 %collective-permute-start = (bf16[1280,512]{1,0:T(8,128)(2,1)S(1)}, bf16[1280,512]{1,0:T(8,128)(2,1)S(1)}, u32[]{:S(2)}, u32[]{:S(2)}) collective-permute-start(bf16[1280,512]{1,0:T(8,128)(2,1)S(1)} %first_moments.1.own), channel_id=1, source_target_pairs={{0,4},{4,0},{8,12},{12,8},{16,20},{20,16},{24,28},{28,24},{32,36},... | collective-permute-start | bytes 3932168 | tf_op jit(solution)/shard_map/ppermute | solution.py:478
  7.4 16.3 %collective-permute-done.8.first = bf16[1280,512]{1,0:T(8,128)(2,1)S(1)} collective-permute-done((bf16[1280,512]{1,0:T(8,128)(2,1)S(1)}, bf16[1280,512]{1,0:T(8,128)(2,1)S(1)}, u32[]{:S(2)}, u32[]{:S(2)}) %collective-permute-start.8) | collective-permute-done | bytes 1310752 | tf_op jit(solution)/shard_map/ppermute | solution.py:478
  23.6 0.0 collective-permute-start.9
  23.6 0.0 collective-permute-done.near
  23.6 2.5 %lifted.1 = (bf16[960,512]{1,0:T(8,128)(2,1)S(1)}, bf16[960,512]{1,0:T(8,128)(2,1)S(1)}, bf16[128,512]{1,0:T(8,128)(2,1)S(1)}, bf16[64,512]{1,0:T(8,128)(2,1)S(1)}) custom-call(bf16[1280,512]{1,0:T(8,128)(2,1)S(1)} %first_moments.1.own, bf16[1280,512]{1,0:T(8,128)(2,1)S(1)} %collective-permute-done.near, bf16[62,4096]{1,0:T(8,128)(2,1)} %top_hbm.1), custom_call_target="tpu_custom_call" | custom-call | tf_op jit(solution)/shard_map/lifted/pallas_call | solution.py:217
  26.2 8.9 %placed_tiles.1 = (bf16[5,1024,1024]{2,1,0:T(8,128)(2,1)S(1)}, bf16[5,512,512]{2,1,0:T(8,128)(2,1)S(1)}, bf16[5,256,256]{2,1,0:T(8,128)(2,1)S(1)}, bf16[5,128,12...) custom-call(s32[1023]{0:T(1024)S(1)} %copy-done, bf16[1023,4096]{1,0:T(8,128)(2,1)} %tail_ref, bf16[1023,4096]{1,0:T(8,128)(2,1)} %tail_ref), custom_call_target="tpu_custom_call" | custom-call | tf_op jit(solution)/shard_map/placed_tiles/pallas_call | solution.py:348
  35.1 3.6 %collective-permute-start.1 = (bf16[1280,512]{1,0:T(8,128)(2,1)S(1)}, bf16[1280,512]{1,0:T(8,128)(2,1)S(1)}, u32[]{:S(2)}, u32[]{:S(2)}) collective-permute-start(bf16[1280,512]{1,0:T(8,128)(2,1)S(1)} %first_moments.1.own), channel_id=1, source_target_pairs={{0,8},{8,16},{12,4},{16,24},{20,12},{24,32},{28,20},{32,40},{36,28... | collective-permute-start | bytes 3932168 | tf_op jit(solution)/shard_map/ppermute | solution.py:478
  38.7 3.5 %collective-permute-start.4 = (bf16[64,512]{1,0:T(8,128)(2,1)S(1)}, bf16[64,512]{1,0:T(8,128)(2,1)S(1)}, u32[]{:S(2)}, u32[]{:S(2)}) collective-permute-start(bf16[64,512]{1,0:T(8,128)(2,1)S(1)} %get-tuple-element.50.mine_ref.t1), channel_id=1, source_target_pairs={{0,24},{4,28},{8,16},{12,20},{16,8},{20,12},{24,0},{28,4},{32,56},... | collective-permute-start | bytes 196616 | tf_op jit(solution)/shard_map/ppermute | solution.py:478
  42.3 1.4 %collective-permute-start.3 = (bf16[64,512]{1,0:T(8,128)(2,1)S(1)}, bf16[64,512]{1,0:T(8,128)(2,1)S(1)}, u32[]{:S(2)}, u32[]{:S(2)}) collective-permute-start(bf16[64,512]{1,0:T(8,128)(2,1)S(1)} %get-tuple-element.50.mine_ref.t1), channel_id=1, source_target_pairs={{0,16},{4,20},{8,24},{12,28},{16,0},{20,4},{24,8},{28,12},{32,48},... | collective-permute-start | bytes 196616 | tf_op jit(solution)/shard_map/ppermute | solution.py:478
  43.6 0.0 collective-permute-start.2
  43.6 16.0 %collective-permute-done.4.third_ref = bf16[64,512]{1,0:T(8,128)(2,1)S(1)} collective-permute-done((bf16[64,512]{1,0:T(8,128)(2,1)S(1)}, bf16[64,512]{1,0:T(8,128)(2,1)S(1)}, u32[]{:S(2)}, u32[]{:S(2)}) %collective-permute-start.4) | collective-permute-done | bytes 65568 | tf_op jit(solution)/shard_map/ppermute | solution.py:478
  59.6 1.5 %collective-permute-done.3.second_ref = bf16[64,512]{1,0:T(8,128)(2,1)S(1)} collective-permute-done((bf16[64,512]{1,0:T(8,128)(2,1)S(1)}, bf16[64,512]{1,0:T(8,128)(2,1)S(1)}, u32[]{:S(2)}, u32[]{:S(2)}) %collective-permute-start.3) | collective-permute-done | bytes 65568 | tf_op jit(solution)/shard_map/ppermute | solution.py:478
  61.1 0.0 collective-permute-done.2.first_ref
  61.1 0.4 shard_map.77
  61.6 0.1 collective-permute-start.7
  61.7 3.6 %collective-permute-start.6 = (bf16[64,512]{1,0:T(8,128)(2,1)S(1)}, bf16[64,512]{1,0:T(8,128)(2,1)S(1)}, u32[]{:S(2)}, u32[]{:S(2)}) collective-permute-start(bf16[64,512]{1,0:T(8,128)(2,1)S(1)} %get-tuple-element.72.mine_ref.t3), channel_id=1, source_target_pairs={{0,64},{4,68},{8,72},{12,76},{16,80},{20,84},{24,88},{28,92},{32,9... | collective-permute-start | bytes 196616 | tf_op jit(solution)/shard_map/ppermute | solution.py:478
  65.3 0.4 collective-permute-start.5
  65.7 7.7 %couple_middle.1.acc = f32[1984,512]{1,0:T(8,128)S(1)} custom-call(bf16[1280,512]{1,0:T(8,128)(2,1)S(1)} %first_moments.1.own, bf16[1280,512]{1,0:T(8,128)(2,1)S(1)} %collective-permute-done.near, bf16[1280,512]{1,0:T(8,128)(2,1)S(1)} %collective-permute-done.8.first, bf16[1280,512]{1,0:T(8,128)(2,1)S(1)} %collective-permute-done.9.third, ...), custom_call_target="tpu_custom_call" | custom-call | tf_op jit(solution)/shard_map/couple_middle/pallas_call | solution.py:440
  73.5 0.0 collective-permute-done.6.second_ref
  73.5 0.4 shard_map.78
  73.9 3.7 %couple_last.1 = (bf16[1984,512]{1,0:T(8,128)(2,1)}, bf16[5,64,512]{2,1,0:T(8,128)(2,1)}) custom-call(bf16[1280,512]{1,0:T(8,128)(2,1)S(1)} %collective-permute-done.1.packet, f32[1984,512]{1,0:T(8,128)S(1)} %couple_middle.1.acc, bf16[64,512]{1,0:T(8,128)(2,1)S(1)} %get-tuple-element.50.mine_ref.t1, bf16[64,512]{1,0:T(8,128)(2,1)S(1)} %get-tuple-element.71.t2, ...), custom_call_target="tpu_custom_call" | custom-call | tf_op jit(solution)/shard_map/couple_last/pallas_call | solution.py:453
  (5 shorter events, 0.0 us)
Async XLA Ops:
  4.1 22.0 %copy-start = (s32[1023]{0:T(1024)S(1)}, s32[1023]{0:T(1024)}, u32[]{:S(2)}) copy-start(s32[1023]{0:T(1024)} %sources.1) | copy-start | bytes 12280
  4.1 19.5 %collective-permute-start.8 = (bf16[1280,512]{1,0:T(8,128)(2,1)S(1)}, bf16[1280,512]{1,0:T(8,128)(2,1)S(1)}, u32[]{:S(2)}, u32[]{:S(2)}) collective-permute-start(bf16[1280,512]{1,0:T(8,128)(2,1)S(1)} %first_moments.1.own), channel_id=1, source_target_pairs={{4,12},{8,0},{12,20},{16,8},{20,28},{24,16},{28,36},{32,24},{36,44... | collective-permute-start | bytes 3932168 | tf_op jit(solution)/shard_map/ppermute | solution.py:478
  5.4 18.2 %collective-permute-start = (bf16[1280,512]{1,0:T(8,128)(2,1)S(1)}, bf16[1280,512]{1,0:T(8,128)(2,1)S(1)}, u32[]{:S(2)}, u32[]{:S(2)}) collective-permute-start(bf16[1280,512]{1,0:T(8,128)(2,1)S(1)} %first_moments.1.own), channel_id=1, source_target_pairs={{0,4},{4,0},{8,12},{12,8},{16,20},{20,16},{24,28},{28,24},{32,36},... | collective-permute-start | bytes 3932168 | tf_op jit(solution)/shard_map/ppermute | solution.py:478
  23.6 42.1 %collective-permute-start.9 = (bf16[1280,512]{1,0:T(8,128)(2,1)S(1)}, bf16[1280,512]{1,0:T(8,128)(2,1)S(1)}, u32[]{:S(2)}, u32[]{:S(2)}) collective-permute-start(bf16[1280,512]{1,0:T(8,128)(2,1)S(1)} %collective-permute-done.8.first), channel_id=1, source_target_pairs={{0,4},{4,0},{8,12},{12,8},{16,20},{20,16},{24,28},{28,24},{32,36},... | collective-permute-start | bytes 3932168 | tf_op jit(solution)/shard_map/ppermute | solution.py:478
  35.1 38.4 %collective-permute-start.1 = (bf16[1280,512]{1,0:T(8,128)(2,1)S(1)}, bf16[1280,512]{1,0:T(8,128)(2,1)S(1)}, u32[]{:S(2)}, u32[]{:S(2)}) collective-permute-start(bf16[1280,512]{1,0:T(8,128)(2,1)S(1)} %first_moments.1.own), channel_id=1, source_target_pairs={{0,8},{8,16},{12,4},{16,24},{20,12},{24,32},{28,20},{32,40},{36,28... | collective-permute-start | bytes 3932168 | tf_op jit(solution)/shard_map/ppermute | solution.py:478
  38.7 20.9 %collective-permute-start.4 = (bf16[64,512]{1,0:T(8,128)(2,1)S(1)}, bf16[64,512]{1,0:T(8,128)(2,1)S(1)}, u32[]{:S(2)}, u32[]{:S(2)}) collective-permute-start(bf16[64,512]{1,0:T(8,128)(2,1)S(1)} %get-tuple-element.50.mine_ref.t1), channel_id=1, source_target_pairs={{0,24},{4,28},{8,16},{12,20},{16,8},{20,12},{24,0},{28,4},{32,56},... | collective-permute-start | bytes 196616 | tf_op jit(solution)/shard_map/ppermute | solution.py:478
  42.3 18.9 %collective-permute-start.3 = (bf16[64,512]{1,0:T(8,128)(2,1)S(1)}, bf16[64,512]{1,0:T(8,128)(2,1)S(1)}, u32[]{:S(2)}, u32[]{:S(2)}) collective-permute-start(bf16[64,512]{1,0:T(8,128)(2,1)S(1)} %get-tuple-element.50.mine_ref.t1), channel_id=1, source_target_pairs={{0,16},{4,20},{8,24},{12,28},{16,0},{20,4},{24,8},{28,12},{32,48},... | collective-permute-start | bytes 196616 | tf_op jit(solution)/shard_map/ppermute | solution.py:478
  43.6 17.5 %collective-permute-start.2 = (bf16[64,512]{1,0:T(8,128)(2,1)S(1)}, bf16[64,512]{1,0:T(8,128)(2,1)S(1)}, u32[]{:S(2)}, u32[]{:S(2)}) collective-permute-start(bf16[64,512]{1,0:T(8,128)(2,1)S(1)} %get-tuple-element.50.mine_ref.t1), channel_id=1, source_target_pairs={{0,8},{4,12},{8,0},{12,4},{16,24},{20,28},{24,16},{28,20},{32,40},... | collective-permute-start | bytes 196616 | tf_op jit(solution)/shard_map/ppermute | solution.py:478
  61.6 11.9 %collective-permute-start.7 = (bf16[64,512]{1,0:T(8,128)(2,1)S(1)}, bf16[64,512]{1,0:T(8,128)(2,1)S(1)}, u32[]{:S(2)}, u32[]{:S(2)}) collective-permute-start(bf16[64,512]{1,0:T(8,128)(2,1)S(1)} %get-tuple-element.72.mine_ref.t3), channel_id=1, source_target_pairs={{0,96},{4,100},{8,104},{12,108},{16,112},{20,116},{24,120},{28,124... | collective-permute-start | bytes 196616 | tf_op jit(solution)/shard_map/ppermute | solution.py:478
  61.7 11.8 %collective-permute-start.6 = (bf16[64,512]{1,0:T(8,128)(2,1)S(1)}, bf16[64,512]{1,0:T(8,128)(2,1)S(1)}, u32[]{:S(2)}, u32[]{:S(2)}) collective-permute-start(bf16[64,512]{1,0:T(8,128)(2,1)S(1)} %get-tuple-element.72.mine_ref.t3), channel_id=1, source_target_pairs={{0,64},{4,68},{8,72},{12,76},{16,80},{20,84},{24,88},{28,92},{32,9... | collective-permute-start | bytes 196616 | tf_op jit(solution)/shard_map/ppermute | solution.py:478
  65.3 8.2 %collective-permute-start.5 = (bf16[64,512]{1,0:T(8,128)(2,1)S(1)}, bf16[64,512]{1,0:T(8,128)(2,1)S(1)}, u32[]{:S(2)}, u32[]{:S(2)}) collective-permute-start(bf16[64,512]{1,0:T(8,128)(2,1)S(1)} %get-tuple-element.72.mine_ref.t3), channel_id=1, source_target_pairs={{0,32},{4,36},{8,40},{12,44},{16,48},{20,52},{24,56},{28,60},{32,0... | collective-permute-start | bytes 196616 | tf_op jit(solution)/shard_map/ppermute | solution.py:478

commit v3 on v2

--- a/solution.py
+++ b/solution.py
@@ -255,6 +255,27 @@
     return CHUNK if k < 10 else 48
 
 
+def crowned(tops, first, second, third, others):
+    def crown_kernel(tops_ref, t1, t2, t3, other_a, other_b, other_c, out_ref):
+        row, column = iotas(RANK, RANK)
+        back = ones_where(natural(column) == row)
+        fourth = ascend(tops_ref, 4, t3[...], other_a[...])
+        side = ascend(tops_ref, 5, other_b[...], other_c[...])
+        fifth = ascend(tops_ref, 6, fourth, side)
+        for k, top in enumerate((t1[...], t2[...], t3[...], fourth, fifth)):
+            out_ref[k] = dot(back, top).astype(BF)
+
+    operands = [on_chip(x) for x in (tops, first, second, third, *others)]
+    return pl.pallas_call(
+        crown_kernel,
+        in_specs=[VMEM_SPEC] * 7,
+        out_specs=VMEM_SPEC,
+        out_shape=jax.ShapeDtypeStruct((5, RANK, PROBES), BF),
+        compiler_params=limit(4),
+        name="crown",
+    )(*operands)
+
+
 def place_kernel(span, sources, tiles_hbm, tail_ref, *refs):
     outs, (tiles_ref, spread_a, spread_b, sems) = refs[:-4], refs[-4:]
     begin, end = span
@@ -403,14 +424,9 @@
 
 
 def last_kernel(
-    packet, acc, t1, t2, t3, t4, t5, d0, d1, d2, d3, d4, out_hbm, tops_hbm, out, tops, up, sems
+    packet, acc, d0, d1, d2, d3, d4, out_hbm, out, up, sems
 ):
-    row, column = iotas(RANK, RANK)
-    back = ones_where(natural(column) == row)
-    for k, top in enumerate((t1, t2, t3, t4, t5)):
-        tops[k] = dot(back, top[...]).astype(BF)
-    copies = [pltpu.make_async_copy(tops, tops_hbm, sems.at[5])]
-    copies[-1].start()
+    copies = []
     piece = piece_of(-2)
 
     def leave(first, size, number):
@@ -448,21 +464,17 @@
     )(*operands)
 
 
-def couple_last(packet, acc, tops, dense):
-    operands = [on_chip(x) for x in (packet, acc, *tops, *dense)]
+def couple_last(packet, acc, dense):
+    operands = [on_chip(x) for x in (packet, acc, *dense)]
     return pl.pallas_call(
         last_kernel,
-        in_specs=[VMEM_SPEC] * 12,
-        out_specs=[HBM_SPEC] * 2,
-        out_shape=[
-            pltpu.HBM((1984, PROBES), BF),
-            pltpu.HBM((5, RANK, PROBES), BF),
-        ],
+        in_specs=[VMEM_SPEC] * 7,
+        out_specs=HBM_SPEC,
+        out_shape=pltpu.HBM((1984, PROBES), BF),
         scratch_shapes=[
             pltpu.VMEM((1984, PROBES), BF),
-            pltpu.VMEM((5, RANK, PROBES), BF),
             pltpu.VMEM((960, PROBES), BF),
-            pltpu.SemaphoreType.DMA((6,)),
+            pltpu.SemaphoreType.DMA((5,)),
         ],
         compiler_params=limit(8),
         name="couple_last",
@@ -498,10 +510,10 @@
     across = [sent(third_top, lambda i: i ^ k) for k in (8, 16, 24)]
     own, relayed, third_top = tied(own, relayed, third_top)
     acc = couple_middle(own, near, inner, relayed, own_up, near_up, dense)
-    outer, across, acc = tied(outer, across, acc)
-    fourth_top, fifth_top = climb(tops, 4, third_top, *across)
-    ladder = (first_top, second_top, third_top, fourth_top, fifth_top)
-    coupled, ancestors = couple_last(outer, acc, ladder, dense)
+    outer, acc = tied(outer, acc)
+    coupled = couple_last(outer, acc, dense)
+    across, coupled = tied(across, coupled)
+    ancestors = crowned(tops, first_top, second_top, third_top, across)
     return coupled.reshape(31, RANK, PROBES), ancestors[None]
 
 

time: 77.9 us -> 76.1 us (0.977)
  starting transfers between devices: 15.9 us -> 14.3 us
  Pallas kernels: 27.1 us -> 27.9 us
  waiting for transfers between devices: 33.8 us -> 33 us
    ppermute x10, starting transfers between devices: 15.9 us -> 14.3 us  [sent(): return lax.ppermute(block, 'leaf', route(step))]
    pallas_call x1 -> x2, Pallas kernels: 3.65 us -> 4.81 us  [the longest x1 3.56 us: couple_last(): pl.pallas_call(last_kernel, in_specs=[VMEM_SPEC] * 7, out_specs=HBM_SPEC,...]
    ppermute x10, waiting for transfers between devices: 33.8 us -> 33 us  [sent(): return lax.ppermute(block, 'leaf', route(step))]
  transfers between devices with their start and end apart: 10 -> 10, of which waited for: 3 -> 4; matrix products, arithmetic and copies ran while one was open for 0% -> 0% of each run, Pallas kernels for 25% -> 31%
where the time goes in v3:
time: 76.1 us; the launch traced here: 75.9 us
  waiting for transfers between devices  33 us (43%)
  Pallas kernels  27.9 us (37%)
  starting transfers between devices  14.3 us (19%)
    ppermute x10, waiting for transfers between devices, sent(): return lax.ppermute(block, 'leaf', route(step))  33 us
    ppermute x10, starting transfers between devices, sent(): return lax.ppermute(block, 'leaf', route(step))  14.3 us
    pallas_call x1, Pallas kernels, placed_tiles(): pl.pallas_call(functools.partial(place_kernel, span), grid=(1,), in_specs...  8.95 us
    pallas_call x1, Pallas kernels, couple_middle(): pl.pallas_call(middle_kernel, in_specs=[VMEM_SPEC] * 11, out_specs=VMEM_S...  7.72 us
    pallas_call x1, Pallas kernels, couple_last(): pl.pallas_call(last_kernel, in_specs=[VMEM_SPEC] * 7, out_specs=HBM_SPEC,...  3.56 us
    pallas_call x1, Pallas kernels, first_moments(): pl.pallas_call(first_kernel, in_specs=[HBM_SPEC] * 3, out_specs=VMEM_SPEC...  3.47 us
    pallas_call x1, Pallas kernels, lifted(): pl.pallas_call(lift_kernel, in_specs=[VMEM_SPEC] * 2 + [HBM_SPEC], out_sp...  2.51 us
  transfers between devices with their start and end apart: 10, of which 4 were waited for; matrix products, arithmetic and copies ran while one was open for 0% of the time, Pallas kernels for 31%

profile of v3, /device:TPU:0, one launch (start us, length us, event | category | flops | bytes accessed | tf_op | source)
XLA Modules:
  0.0 75.9 jit_solution(11134307979764210193)
XLA Ops:
  0.6 3.5 %first_moments.1.own = bf16[1280,512]{1,0:T(8,128)(2,1)S(1)} custom-call(bf16[4096,512]{1,0:T(8,128)(2,1)} %points_hbm.1, bf16[16,64,256]{2,1,0:T(8,128)(2,1)} %basis_hbm.1, bf16[30,4096]{1,0:T(8,128)(2,1)} %links_hbm.1), custom_call_target="tpu_custom_call" | custom-call | tf_op jit(solution)/shard_map/first_moments/pallas_call | solution.py:129
  4.1 0.0 copy-start
  4.1 0.1 collective-permute-start
  4.2 1.3 %collective-permute-start.8 = (bf16[1280,512]{1,0:T(8,128)(2,1)S(1)}, bf16[1280,512]{1,0:T(8,128)(2,1)S(1)}, u32[]{:S(2)}, u32[]{:S(2)}) collective-permute-start(bf16[1280,512]{1,0:T(8,128)(2,1)S(1)} %first_moments.1.own), channel_id=1, source_target_pairs={{4,12},{8,0},{12,20},{16,8},{20,28},{24,16},{28,36},{32,24},{36,44... | collective-permute-start | bytes 3932168 | tf_op jit(solution)/shard_map/ppermute | solution.py:490
  5.5 1.7 %collective-permute-done.near = bf16[1280,512]{1,0:T(8,128)(2,1)S(1)} collective-permute-done((bf16[1280,512]{1,0:T(8,128)(2,1)S(1)}, bf16[1280,512]{1,0:T(8,128)(2,1)S(1)}, u32[]{:S(2)}, u32[]{:S(2)}) %collective-permute-start) | collective-permute-done | bytes 1310752 | tf_op jit(solution)/shard_map/ppermute | solution.py:490
  7.2 2.5 %lifted.1 = (bf16[960,512]{1,0:T(8,128)(2,1)S(1)}, bf16[960,512]{1,0:T(8,128)(2,1)S(1)}, bf16[128,512]{1,0:T(8,128)(2,1)S(1)}, bf16[64,512]{1,0:T(8,128)(2,1)S(1)}) custom-call(bf16[1280,512]{1,0:T(8,128)(2,1)S(1)} %first_moments.1.own, bf16[1280,512]{1,0:T(8,128)(2,1)S(1)} %collective-permute-done.near, bf16[62,4096]{1,0:T(8,128)(2,1)} %top_hbm.1), custom_call_target="tpu_custom_call" | custom-call | tf_op jit(solution)/shard_map/lifted/pallas_call | solution.py:217
  9.8 14.0 %collective-permute-done.8.first = bf16[1280,512]{1,0:T(8,128)(2,1)S(1)} collective-permute-done((bf16[1280,512]{1,0:T(8,128)(2,1)S(1)}, bf16[1280,512]{1,0:T(8,128)(2,1)S(1)}, u32[]{:S(2)}, u32[]{:S(2)}) %collective-permute-start.8) | collective-permute-done | bytes 1310752 | tf_op jit(solution)/shard_map/ppermute | solution.py:490
  23.7 9.0 %placed_tiles.1 = (bf16[5,1024,1024]{2,1,0:T(8,128)(2,1)S(1)}, bf16[5,512,512]{2,1,0:T(8,128)(2,1)S(1)}, bf16[5,256,256]{2,1,0:T(8,128)(2,1)S(1)}, bf16[5,128,12...) custom-call(s32[1023]{0:T(1024)S(1)} %copy-done, bf16[1023,4096]{1,0:T(8,128)(2,1)} %tail_ref, bf16[1023,4096]{1,0:T(8,128)(2,1)} %tail_ref), custom_call_target="tpu_custom_call" | custom-call | tf_op jit(solution)/shard_map/placed_tiles/pallas_call | solution.py:369
  32.7 3.6 %collective-permute-start.7 = (bf16[1280,512]{1,0:T(8,128)(2,1)S(1)}, bf16[1280,512]{1,0:T(8,128)(2,1)S(1)}, u32[]{:S(2)}, u32[]{:S(2)}) collective-permute-start(bf16[1280,512]{1,0:T(8,128)(2,1)S(1)} %first_moments.1.own), channel_id=1, source_target_pairs={{0,8},{8,16},{12,4},{16,24},{20,12},{24,32},{28,20},{32,40},{36,28... | collective-permute-start | bytes 3932168 | tf_op jit(solution)/shard_map/ppermute | solution.py:490
  36.3 4.2 %collective-permute-start.3 = (bf16[64,512]{1,0:T(8,128)(2,1)S(1)}, bf16[64,512]{1,0:T(8,128)(2,1)S(1)}, u32[]{:S(2)}, u32[]{:S(2)}) collective-permute-start(bf16[64,512]{1,0:T(8,128)(2,1)S(1)} %get-tuple-element.40.mine_ref.t1), channel_id=1, source_target_pairs={{0,24},{4,28},{8,16},{12,20},{16,8},{20,12},{24,0},{28,4},{32,56},... | collective-permute-start | bytes 196616 | tf_op jit(solution)/shard_map/ppermute | solution.py:490
  40.5 0.7 collective-permute-start.2
  41.2 0.2 collective-permute-start.1
  41.4 15.9 %collective-permute-done.3.third_ref = bf16[64,512]{1,0:T(8,128)(2,1)S(1)} collective-permute-done((bf16[64,512]{1,0:T(8,128)(2,1)S(1)}, bf16[64,512]{1,0:T(8,128)(2,1)S(1)}, u32[]{:S(2)}, u32[]{:S(2)}) %collective-permute-start.3) | collective-permute-done | bytes 65568 | tf_op jit(solution)/shard_map/ppermute | solution.py:490
  57.4 1.4 %collective-permute-done.2.second_ref = bf16[64,512]{1,0:T(8,128)(2,1)S(1)} collective-permute-done((bf16[64,512]{1,0:T(8,128)(2,1)S(1)}, bf16[64,512]{1,0:T(8,128)(2,1)S(1)}, u32[]{:S(2)}, u32[]{:S(2)}) %collective-permute-start.2) | collective-permute-done | bytes 65568 | tf_op jit(solution)/shard_map/ppermute | solution.py:490
  58.7 0.0 collective-permute-done.1.first_ref
  58.7 0.4 shard_map.77
  59.1 0.3 collective-permute-start.6
  59.4 3.5 %collective-permute-start.5 = (bf16[64,512]{1,0:T(8,128)(2,1)S(1)}, bf16[64,512]{1,0:T(8,128)(2,1)S(1)}, u32[]{:S(2)}, u32[]{:S(2)}) collective-permute-start(bf16[64,512]{1,0:T(8,128)(2,1)S(1)} %get-tuple-element.70.t3), channel_id=1, source_target_pairs={{0,64},{4,68},{8,72},{12,76},{16,80},{20,84},{24,88},{28,92},{32,9... | collective-permute-start | bytes 196616 | tf_op jit(solution)/shard_map/ppermute | solution.py:490
  62.9 0.4 collective-permute-start.4
  63.3 0.0 collective-permute-done.9.third
  63.3 7.7 %couple_middle.1.acc = f32[1984,512]{1,0:T(8,128)S(1)} custom-call(bf16[1280,512]{1,0:T(8,128)(2,1)S(1)} %first_moments.1.own, bf16[1280,512]{1,0:T(8,128)(2,1)S(1)} %collective-permute-done.near, bf16[1280,512]{1,0:T(8,128)(2,1)S(1)} %collective-permute-done.8.first, bf16[1280,512]{1,0:T(8,128)(2,1)S(1)} %collective-permute-done.9.third, ...), custom_call_target="tpu_custom_call" | custom-call | tf_op jit(solution)/shard_map/couple_middle/pallas_call | solution.py:456
  71.0 0.0 collective-permute-done.7.packet
  71.0 3.6 %couple_last.1 = bf16[1984,512]{1,0:T(8,128)(2,1)} custom-call(bf16[1280,512]{1,0:T(8,128)(2,1)S(1)} %collective-permute-done.7.packet, f32[1984,512]{1,0:T(8,128)S(1)} %couple_middle.1.acc, bf16[5,1024,1024]{2,1,0:T(8,128)(2,1)S(1)} %get-tuple-element.61.d0, bf16[5,512,512]{2,1,0:T(8,128)(2,1)S(1)} %get-tuple-element.62.d1, ...), custom_call_target="tpu_custom_call" | custom-call | tf_op jit(solution)/shard_map/couple_last/pallas_call | solution.py:469
  74.6 1.2 %crown.1 = bf16[5,64,512]{2,1,0:T(8,128)(2,1)} custom-call(bf16[128,512]{1,0:T(8,128)(2,1)S(1)} %get-tuple-element.38.tops_ref, bf16[64,512]{1,0:T(8,128)(2,1)S(1)} %get-tuple-element.40.mine_ref.t1, bf16[64,512]{1,0:T(8,128)(2,1)S(1)} %get-tuple-element.69.t2, bf16[64,512]{1,0:T(8,128)(2,1)S(1)} %get-tuple-element.70.t3, ...), custom_call_target="tpu_custom_call" | custom-call | tf_op jit(solution)/shard_map/crown/pallas_call | solution.py:269
  (5 shorter events, 0.0 us)
Async XLA Ops:
  4.1 19.6 %copy-start = (s32[1023]{0:T(1024)S(1)}, s32[1023]{0:T(1024)}, u32[]{:S(2)}) copy-start(s32[1023]{0:T(1024)} %sources.1) | copy-start | bytes 12280
  4.1 3.1 %collective-permute-start = (bf16[1280,512]{1,0:T(8,128)(2,1)S(1)}, bf16[1280,512]{1,0:T(8,128)(2,1)S(1)}, u32[]{:S(2)}, u32[]{:S(2)}) collective-permute-start(bf16[1280,512]{1,0:T(8,128)(2,1)S(1)} %first_moments.1.own), channel_id=1, source_target_pairs={{0,4},{4,0},{8,12},{12,8},{16,20},{20,16},{24,28},{28,24},{32,36},... | collective-permute-start | bytes 3932168 | tf_op jit(solution)/shard_map/ppermute | solution.py:490
  4.2 19.5 %collective-permute-start.8 = (bf16[1280,512]{1,0:T(8,128)(2,1)S(1)}, bf16[1280,512]{1,0:T(8,128)(2,1)S(1)}, u32[]{:S(2)}, u32[]{:S(2)}) collective-permute-start(bf16[1280,512]{1,0:T(8,128)(2,1)S(1)} %first_moments.1.own), channel_id=1, source_target_pairs={{4,12},{8,0},{12,20},{16,8},{20,28},{24,16},{28,36},{32,24},{36,44... | collective-permute-start | bytes 3932168 | tf_op jit(solution)/shard_map/ppermute | solution.py:490
  23.7 39.6 %collective-permute-start.9 = (bf16[1280,512]{1,0:T(8,128)(2,1)S(1)}, bf16[1280,512]{1,0:T(8,128)(2,1)S(1)}, u32[]{:S(2)}, u32[]{:S(2)}) collective-permute-start(bf16[1280,512]{1,0:T(8,128)(2,1)S(1)} %collective-permute-done.8.first), channel_id=1, source_target_pairs={{0,4},{4,0},{8,12},{12,8},{16,20},{20,16},{24,28},{28,24},{32,36},... | collective-permute-start | bytes 3932168 | tf_op jit(solution)/shard_map/ppermute | solution.py:490
  32.7 38.4 %collective-permute-start.7 = (bf16[1280,512]{1,0:T(8,128)(2,1)S(1)}, bf16[1280,512]{1,0:T(8,128)(2,1)S(1)}, u32[]{:S(2)}, u32[]{:S(2)}) collective-permute-start(bf16[1280,512]{1,0:T(8,128)(2,1)S(1)} %first_moments.1.own), channel_id=1, source_target_pairs={{0,8},{8,16},{12,4},{16,24},{20,12},{24,32},{28,20},{32,40},{36,28... | collective-permute-start | bytes 3932168 | tf_op jit(solution)/shard_map/ppermute | solution.py:490
  36.3 21.1 %collective-permute-start.3 = (bf16[64,512]{1,0:T(8,128)(2,1)S(1)}, bf16[64,512]{1,0:T(8,128)(2,1)S(1)}, u32[]{:S(2)}, u32[]{:S(2)}) collective-permute-start(bf16[64,512]{1,0:T(8,128)(2,1)S(1)} %get-tuple-element.40.mine_ref.t1), channel_id=1, source_target_pairs={{0,24},{4,28},{8,16},{12,20},{16,8},{20,12},{24,0},{28,4},{32,56},... | collective-permute-start | bytes 196616 | tf_op jit(solution)/shard_map/ppermute | solution.py:490
  40.5 18.2 %collective-permute-start.2 = (bf16[64,512]{1,0:T(8,128)(2,1)S(1)}, bf16[64,512]{1,0:T(8,128)(2,1)S(1)}, u32[]{:S(2)}, u32[]{:S(2)}) collective-permute-start(bf16[64,512]{1,0:T(8,128)(2,1)S(1)} %get-tuple-element.40.mine_ref.t1), channel_id=1, source_target_pairs={{0,16},{4,20},{8,24},{12,28},{16,0},{20,4},{24,8},{28,12},{32,48},... | collective-permute-start | bytes 196616 | tf_op jit(solution)/shard_map/ppermute | solution.py:490
  41.2 17.5 %collective-permute-start.1 = (bf16[64,512]{1,0:T(8,128)(2,1)S(1)}, bf16[64,512]{1,0:T(8,128)(2,1)S(1)}, u32[]{:S(2)}, u32[]{:S(2)}) collective-permute-start(bf16[64,512]{1,0:T(8,128)(2,1)S(1)} %get-tuple-element.40.mine_ref.t1), channel_id=1, source_target_pairs={{0,8},{4,12},{8,0},{12,4},{16,24},{20,28},{24,16},{28,20},{32,40},... | collective-permute-start | bytes 196616 | tf_op jit(solution)/shard_map/ppermute | solution.py:490
  59.1 15.5 %collective-permute-start.6 = (bf16[64,512]{1,0:T(8,128)(2,1)S(1)}, bf16[64,512]{1,0:T(8,128)(2,1)S(1)}, u32[]{:S(2)}, u32[]{:S(2)}) collective-permute-start(bf16[64,512]{1,0:T(8,128)(2,1)S(1)} %get-tuple-element.70.t3), channel_id=1, source_target_pairs={{0,96},{4,100},{8,104},{12,108},{16,112},{20,116},{24,120},{28,124... | collective-permute-start | bytes 196616 | tf_op jit(solution)/shard_map/ppermute | solution.py:490
  59.4 15.2 %collective-permute-start.5 = (bf16[64,512]{1,0:T(8,128)(2,1)S(1)}, bf16[64,512]{1,0:T(8,128)(2,1)S(1)}, u32[]{:S(2)}, u32[]{:S(2)}) collective-permute-start(bf16[64,512]{1,0:T(8,128)(2,1)S(1)} %get-tuple-element.70.t3), channel_id=1, source_target_pairs={{0,64},{4,68},{8,72},{12,76},{16,80},{20,84},{24,88},{28,92},{32,9... | collective-permute-start | bytes 196616 | tf_op jit(solution)/shard_map/ppermute | solution.py:490
  62.9 11.7 %collective-permute-start.4 = (bf16[64,512]{1,0:T(8,128)(2,1)S(1)}, bf16[64,512]{1,0:T(8,128)(2,1)S(1)}, u32[]{:S(2)}, u32[]{:S(2)}) collective-permute-start(bf16[64,512]{1,0:T(8,128)(2,1)S(1)} %get-tuple-element.70.t3), channel_id=1, source_target_pairs={{0,32},{4,36},{8,40},{12,44},{16,48},{20,52},{24,56},{28,60},{32,0... | collective-permute-start | bytes 196616 | tf_op jit(solution)/shard_map/ppermute | solution.py:490
